TPU v7x, 256 devices: a whole 4x4x8 slice. The times are simulated.
256 devices in a mesh: gx: 16 (over y_lo, z), gy: 16 (over y_hi, x, core).
Axes of the slice: x: 4, y: 4 (y_hi: 2, y_lo: 2; y = y_hi * 2 + y_lo), z: 8, core: 2. Of those that a mesh axis runs over, the one named last changes fastest.
Arguments:
- obs_values: bfloat16 [4096, 48, 128], P(('gx', 'gy')), may hold values from -1.5 to 1.5
- obs_weight: float32 [4096, 128], P(('gx', 'gy')), may hold values from 0.25 to 4
- obs_box: int32 [4096, 128], P(('gx', 'gy')), may hold values from 0 to 127
- obs_owner: int32 [4096], P(('gx', 'gy')), may hold values from 0 to 255
- block_count: int32 [256], P(('gx', 'gy')), may hold values from 1 to 16, as said below
- diff_x: float32 [48, 128, 2048], P(None, 'gx', 'gy'), may hold values from 0.02 to 0.24
- diff_y: float32 [48, 128, 2048], P(None, 'gx', 'gy'), may hold values from 0.02 to 0.24
- spread_std: float32 [48, 128, 2048], P(None, 'gx', 'gy'), may hold values from 0.3 to 3
- land_sea: int32 [128, 2048], P('gx', 'gy'), may hold values 0 or 1
- vert_corr: float32 [48, 48], replicated, may hold values from -0.12268693 to 1.122687, as said below
Outputs:
- increment: float32 [48, 128, 2048], P(None, 'gx', 'gy')
Inputs may be any that keep to these rules, and one draw needn't show every extreme that they name: `block_count`: some device holds exactly 16 filled blocks in every draw. vert_corr is the identity plus a matrix E whose entries have magnitude at most 0.85 / sqrt(48); it is the same for all columns.
All inputs are finite; a program needn't handle non-finite values. No bound on the sum of `land_sea` on one device may be relied on, other than what follows from the above.
Results may differ from a plain program's by a relative error of at most 0.0003.
Values sent between devices are 32-bit elements; how exact they have to be, the bound alone decides.
A program may use at most 64 MiB of HBM per device.

v0:
```python
import jax
import jax.numpy as jnp
from jax import lax
from jax.sharding import PartitionSpec as P

BOX_DEV = 128
PASSES = 4


HIGH = lax.Precision.HIGHEST


def extended(block, sides, width):
    for axis, dim in sides:
        count = lax.axis_size(axis)
        forward = [(i, i + 1) for i in range(count - 1)]
        forward.append((count - 1, 0))
        backward = [(target, source) for source, target in forward]
        low = lax.ppermute(
            lax.slice_in_dim(block, block.shape[dim] - width, None, axis=dim), axis, forward
        )
        high = lax.ppermute(lax.slice_in_dim(block, 0, width, axis=dim), axis, backward)
        block = jnp.concatenate([low, block, high], axis=dim)
    return block


def one_pass(field, east, north):
    centre = field[:, 1:-1, 1:-1]
    out = centre + east[:, 1:-1, 1:-1] * (field[:, 2:, 1:-1] - centre)
    out = out + east[:, :-2, 1:-1] * (field[:, :-2, 1:-1] - centre)
    out = out + north[:, 1:-1, 1:-1] * (field[:, 1:-1, 2:] - centre)
    out = out + north[:, 1:-1, :-2] * (field[:, 1:-1, :-2] - centre)
    return out


def face_terms(padded, levels):
    diff_east = padded[:levels]
    diff_north = padded[levels : 2 * levels]
    mask = padded[2 * levels]
    east = diff_east[:, :-1, :] * (mask[:-1, :] * mask[1:, :])[None]
    north = diff_north[:, :, :-1] * (mask[:, :-1] * mask[:, 1:])[None]
    east = jnp.pad(east, ((0, 0), (0, 1), (0, 0)))
    north = jnp.pad(north, ((0, 0), (0, 0), (0, 1)))
    return (east, north)


def passes_round(padded, east, north):
    padded = one_pass(padded, east, north)
    return padded


def local(
    obs_values,
    obs_weight,
    obs_box,
    obs_owner,
    block_count,
    diff_x,
    diff_y,
    spread_std,
    land_sea,
    vert_corr,
):
    levels = diff_x.shape[0]
    width_x = diff_x.shape[1]
    width_y = diff_x.shape[2]
    blocks = obs_values.shape[0]
    box_count = BOX_DEV
    filled = (jnp.arange(blocks, dtype=jnp.int32) < block_count[0]).astype(jnp.float32)
    weighted = obs_values.astype(jnp.float32) * (obs_weight * filled[:, None])[:, None, :]
    onehot = (obs_box[:, :, None] == jnp.arange(box_count, dtype=jnp.int32)[None, None, :]).astype(
        jnp.float32
    )
    contrib = jnp.einsum("blo,bok->blk", weighted, onehot, precision=HIGH)
    targets = jnp.arange(lax.axis_size(("gx", "gy")) * 1, dtype=jnp.int32)
    select = (obs_owner[None, :] == targets[:, None]).astype(jnp.float32)
    superob = lax.psum_scatter(
        jnp.einsum("rb,blk->rlk", select, contrib, precision=HIGH),
        ("gx", "gy"),
        scatter_dimension=0,
        tiled=True,
    )[0]
    vbox = jnp.dot(vert_corr, superob, precision=HIGH)
    spread = vbox.reshape(levels, 8, 16)
    spread = jnp.repeat(jnp.repeat(spread, width_x // 8, axis=1), width_y // 16, axis=2)
    mask = land_sea.astype(jnp.float32)
    forcing = spread * spread_std * mask[None]
    depth = 1
    rounds = PASSES // depth
    moved = lax.all_to_all(
        jnp.stack([diff_x, diff_y]), "gy", split_axis=1, concat_axis=3, tiled=True
    )
    mask_whole = lax.all_gather(mask, "gy", axis=1, tiled=True)
    field = lax.all_to_all(forcing, "gy", split_axis=0, concat_axis=2, tiled=True)
    group = field.shape[0]
    stacked = jnp.concatenate([moved[0], moved[1], mask_whole[None]], axis=0)
    stacked = extended(stacked, (("gx", 1),), depth)
    stacked = jnp.pad(stacked, ((0, 0), (0, 0), (depth, depth)))
    east, north = face_terms(stacked, group)
    for turn in range(rounds):
        padded = extended(field, (("gx", 1),), depth)
        padded = jnp.pad(padded, ((0, 0), (0, 0), (depth, depth)))
        field = passes_round(padded, east, north)
    field = lax.all_to_all(field, "gy", split_axis=2, concat_axis=0, tiled=True)
    mixed = jnp.dot(vert_corr, field.reshape(levels, -1), precision=HIGH).reshape(
        levels, width_x, width_y
    )
    return mixed * spread_std * mask[None]


def solution(mesh):
    in_specs = (
        P(("gx", "gy"), None, None),
        P(("gx", "gy"), None),
        P(("gx", "gy"), None),
        P(("gx", "gy")),
        P(("gx", "gy")),
        P(None, "gx", "gy"),
        P(None, "gx", "gy"),
        P(None, "gx", "gy"),
        P("gx", "gy"),
        P(),
    )
    out_specs = P(None, "gx", "gy")
    return jax.shard_map(local, mesh=mesh, in_specs=in_specs, out_specs=out_specs, check_vma=False)
```

profile of v0, /device:TPU:1, one launch (start us, length us, event | category | flops | bytes accessed | tf_op | source)
XLA Modules:
  0.0 1416.2 jit_solution(16087760132111808996)
XLA Ops:
  8.0 1.7 fusion
  9.7 3.4 fusion.4
  13.0 6.3 copy.42
  21.1 8.4 all-to-all-start.1
  29.6 24.6 %all_gather.3 = f32[8,2048]{1,0:T(8,128)S(1)} all-gather(f32[8,128]{1,0:T(8,128)S(1)} %convert_element_type.28), channel_id=1, replica_groups=mesh['gx'=16,'gy'=16] {'gy'}, dimensions={1}, use_global_device_ids=true | all-gather | bytes 69632 | tf_op jit(solution)/shard_map/all_gather | solution.py:93
  54.5 5.8 collective-permute-start.1
  60.3 1.3 collective-permute-done.1
  61.5 3.9 collective-permute-done
  66.2 1230.5 %reduce-scatter.2.cloned.1.call-done = f32[1,48,128]{2,1,0:T(8,128)} async-done(((f32[256,48,128]{2,1,0:T(8,128)}), f32[1,48,128]{2,1,0:T(8,128)}) %reduce-scatter.2.cloned.1.call-update) | async-done | bytes 24592 | tf_op jit(solution)/shard_map/reduce_scatter | solution.py:77
  1298.6 10.0 all-to-all-start
  1308.6 8.2 all-to-all-done
  1316.9 1.5 collective-permute-start.3
  1319.6 2.4 collective-permute-done.3
  1322.7 1.5 collective-permute-start.5
  1325.4 35.4 %collective-permute-done.5 = f32[3,1,2048]{2,1,0:T(1,128)S(1)} collective-permute-done((f32[3,1,2048]{2,1,0:T(1,128)S(1)}, f32[3,1,2048]{2,1,0:T(1,128)S(1)}, u32[]{:S(2)}, u32[]{:S(2)}) %collective-permute-start.5) | collective-permute-done | bytes 24608 | tf_op jit(solution)/shard_map/ppermute | solution.py:19
  1361.5 1.8 collective-permute-start.6
  1364.2 3.8 collective-permute-done.7
  1370.2 1.5 collective-permute-done.8
  1371.7 2.4 collective-permute-done.9
  1374.8 3.0 copy.47
  1377.8 4.4 reshape.30
  1382.2 17.1 %all_to_all.48 = f32[16,1,3072]{2,1,0:T(1,128)S(1)} all-to-all(f32[16,1,3072]{2,1,0:T(1,128)S(1)} %reshape.30), channel_id=1, replica_groups=mesh['gx'=16,'gy'=16] {'gy'}, dimensions={0} | all-to-all | bytes 393216 | tf_op jit(solution)/shard_map/all_to_all | solution.py:104
  1400.9 4.0 reshape.31
  1405.0 3.3 copy.48
  (60 shorter events, 16.1 us)
Async XLA Ops:
  6.5 1290.1 %copy-start = (f32[48,48]{1,0:T(8,128)S(1)}, f32[48,48]{1,0:T(8,128)}, u32[]{:S(2)}) copy-start(f32[48,48]{1,0:T(8,128)} %param.19) | copy-start | bytes 27652
  6.5 1290.1 %reduce-scatter.2.cloned.1.call-start = ((), (), s32[]{:S(2)}) async-start(), calls=%async_computation.4 | async-start | bytes 6316032 | tf_op jit(solution)/shard_map/reduce_scatter | solution.py:77
  19.3 0.9 copy-start.2
  19.3 1.0 copy-start.3
  19.3 10.2 copy-start.4
  19.3 1278.5 %copy-start.1 = (f32[48,8,128]{2,1,0:T(8,128)S(1)}, f32[48,8,128]{2,1,0:T(8,128)}, u32[]{:S(2)}) copy-start(f32[48,8,128]{2,1,0:T(8,128)} %param.17) | copy-start | bytes 589828
  21.1 33.1 %all-to-all-start.1 = ((f32[2,48,8,128]{3,2,0,1:T(8,128)}), f32[2,48,8,128]{3,2,0,1:T(8,128)S(1)}, u32[]{:S(2)}, u32[]{:S(2)}) async-start(f32[2,48,8,128]{3,2,0,1:T(8,128)} %pad_maximum_fusion), calls=%async_computation.2 | async-start | bytes 786432 | tf_op jit(solution)/shard_map/all_to_all | solution.py:90
  54.5 7.0 collective-permute-start.1
  60.3 5.1 collective-permute-start
  1298.6 18.2 %all-to-all-start = ((f32[48,8,128]{2,1,0:T(8,128)}), f32[48,8,128]{2,1,0:T(8,128)S(1)}, u32[]{:S(2)}, u32[]{:S(2)}) async-start(f32[48,8,128]{2,1,0:T(8,128)} %multiply_multiply_fusion), calls=%async_computation.1 | async-start | bytes 393216 | tf_op jit(solution)/shard_map/all_to_all | solution.py:94
  1316.8 2.8 collective-permute-start.2
  1316.9 5.0 collective-permute-start.3
  1322.6 2.8 collective-permute-start.4
  1322.7 38.0 %collective-permute-start.5 = (f32[3,1,2048]{2,1,0:T(1,128)S(1)}, f32[3,1,2048]{2,1,0:T(1,128)S(1)}, u32[]{:S(2)}, u32[]{:S(2)}) collective-permute-start(f32[3,1,2048]{2,1,0:T(1,128)S(1)} %get-tuple-element.13), channel_id=1, source_target_pairs={{0,16},{16,32},{32,48},{48,64},{64,80},{80,96},{96,112},{112,128},... | collective-permute-start | bytes 73736 | tf_op jit(solution)/shard_map/ppermute | solution.py:19
  1361.5 2.8 collective-permute-start.6
  1363.2 4.8 collective-permute-start.7
  1368.7 3.0 collective-permute-start.8
  1369.3 4.8 collective-permute-start.9
Sparse Core Ops, SparseCore 0:
  19.5 1277.0 reduce-scatter.1
where the time goes:
time: 1420 us
  waiting for transfers between devices  1290 us (91%)
  blocking collectives  41.7 us (3%)
  starting transfers between devices  30.5 us (2%)
  local copies, waits for them, and re-layouts  23.4 us (2%)
  between operations  14.3 us (1%)
    reduce_scatter x1, waiting for transfers between devices, local(): lax.psum_scatter(jnp.einsum('rb,blk->rlk', select, contrib, precision=HIG...  1230 us
    ppermute x5, waiting for transfers between devices, extended(): lax.ppermute(lax.slice_in_dim(block, block.shape[dim] - width, None, axis...  47.8 us
  transfers between devices with their start and end apart: 13, of which 12 were waited for; matrix products, arithmetic and copies ran while one was open for 0% of the time, Pallas kernels for 0%

commit v1 on v0

--- a/solution.py
+++ b/solution.py
@@ -72,14 +72,13 @@
         jnp.float32
     )
     contrib = jnp.einsum("blo,bok->blk", weighted, onehot, precision=HIGH)
+    by_level = lax.all_to_all(contrib, "gy", split_axis=1, concat_axis=0, tiled=True)
+    owners = lax.all_gather(obs_owner, "gy", axis=0, tiled=True)
     targets = jnp.arange(lax.axis_size(("gx", "gy")) * 1, dtype=jnp.int32)
-    select = (obs_owner[None, :] == targets[:, None]).astype(jnp.float32)
-    superob = lax.psum_scatter(
-        jnp.einsum("rb,blk->rlk", select, contrib, precision=HIGH),
-        ("gx", "gy"),
-        scatter_dimension=0,
-        tiled=True,
-    )[0]
+    select = (owners[None, :] == targets[:, None]).astype(jnp.float32)
+    partial = jnp.einsum("rb,blk->rlk", select, by_level, precision=HIGH)
+    mine = lax.psum_scatter(partial, "gx", scatter_dimension=0, tiled=True)
+    superob = lax.all_to_all(mine, "gy", split_axis=0, concat_axis=1, tiled=True)[0]
     vbox = jnp.dot(vert_corr, superob, precision=HIGH)
     spread = vbox.reshape(levels, 8, 16)
     spread = jnp.repeat(jnp.repeat(spread, width_x // 8, axis=1), width_y // 16, axis=2)

time: 1420 us -> 237 us (0.17)
  waiting for transfers between devices: 1290 us -> 89.4 us
  starting transfers between devices: 30.5 us -> 47.9 us
    reduce_scatter x1, waiting for transfers between devices: 1230 us -> 56.3 us  [local(): mine = lax.psum_scatter(partial, 'gx', scatter_dimension=0, tiled=True)]
    ppermute x5, waiting for transfers between devices: 47.8 us -> 9.05 us  [extended(): lax.ppermute(lax.slice_in_dim(block, block.shape[dim] - width, None, axis...]
    all_to_all x0 -> x2, starting transfers between devices: none -> 23.7 us  [the longest x1 19.3 us: local(): lax.all_to_all(mine, 'gy', split_axis=0, concat_axis=1, tiled=True)[0]]
  transfers between devices with their start and end apart: 13 -> 15, of which waited for: 12 -> 12; matrix products, arithmetic and copies ran while one was open for 0% -> 4% of each run, Pallas kernels for 0% -> 0%
where the time goes in v1:
time: 237 us; the launch traced here: 236 us
  waiting for transfers between devices  89.4 us (38%)
  blocking collectives  50.5 us (21%)
  starting transfers between devices  47.9 us (20%)
  local copies, waits for them, and re-layouts  20.5 us (9%)
  between operations  15 us (6%)
  other arithmetic  9.19 us (4%)
  matrix products  3.35 us (1%)
    reduce_scatter x1, waiting for transfers between devices, local(): mine = lax.psum_scatter(partial, 'gx', scatter_dimension=0, tiled=True)  56.3 us
    all_gather x1, blocking collectives, local(): mask_whole = lax.all_gather(mask, 'gy', axis=1, tiled=True)  22.7 us
    all_to_all x1, starting transfers between devices, local(): lax.all_to_all(mine, 'gy', split_axis=0, concat_axis=1, tiled=True)[0]  19.3 us
    all_to_all x1, blocking collectives, local(): field = lax.all_to_all(field, 'gy', split_axis=2, concat_axis=0, tiled=True)  16.5 us
    unnamed x1, blocking collectives  11.3 us
    unnamed x10, local copies, waits for them, and re-layouts  10.7 us
    ppermute x5, waiting for transfers between devices, extended(): lax.ppermute(lax.slice_in_dim(block, block.shape[dim] - width, None, axis...  9.05 us
    all_to_all x1, starting transfers between devices, local(): lax.all_to_all(jnp.stack([diff_x, diff_y]), 'gy', split_axis=1, concat_ax...  8.45 us
  transfers between devices with their start and end apart: 15, of which 12 were waited for; matrix products, arithmetic and copies ran while one was open for 4% of the time, Pallas kernels for 0%

profile of v1, /device:TPU:1, one launch (start us, length us, event | category | flops | bytes accessed | tf_op | source)
XLA Modules:
  0.0 235.9 jit_solution(9146900084684502872)
XLA Ops:
  6.5 1.8 pad_maximum_fusion
  8.3 8.4 %all-to-all-start.3 = ((f32[2,48,8,128]{3,2,0,1:T(8,128)}), f32[2,48,8,128]{3,2,0,1:T(8,128)S(1)}, u32[]{:S(2)}, u32[]{:S(2)}) async-start(f32[2,48,8,128]{3,2,0,1:T(8,128)} %pad_maximum_fusion), calls=%async_computation.4 | async-start | bytes 786432 | tf_op jit(solution)/shard_map/all_to_all | solution.py:89
  18.9 1.7 fusion
  24.2 11.3 %all-reduce.5 = s32[256]{0:T(256)S(1)} all-reduce(s32[256]{0:T(256)S(1)} %dynamic-update-slice), channel_id=1, replica_groups=mesh['gx'=16,'gy'=16] {'gy'}, use_global_device_ids=true, to_apply=%add.5 | all-reduce | flops 256 | bytes 2048
  35.5 22.7 %all_gather.7 = f32[8,2048]{1,0:T(8,128)S(1)} all-gather(f32[8,128]{1,0:T(8,128)S(1)} %convert_element_type.28), channel_id=1, replica_groups=mesh['gx'=16,'gy'=16] {'gy'}, dimensions={1}, use_global_device_ids=true | all-gather | bytes 69632 | tf_op jit(solution)/shard_map/all_gather | solution.py:92
  58.3 4.4 %all-to-all-start = ((f32[16,48,128]{2,0,1:T(8,128)}), f32[16,48,128]{2,0,1:T(8,128)S(1)}, u32[]{:S(2)}, u32[]{:S(2)}) async-start(f32[16,48,128]{2,0,1:T(8,128)} %copy.48), calls=%async_computation | async-start | bytes 786432 | tf_op jit(solution)/shard_map/all_to_all | solution.py:75
  63.1 1.7 collective-permute-start
  64.8 4.1 %collective-permute-start.1 = (f32[7,1,2048]{2,1,0:T(1,128)S(1)}, f32[7,1,2048]{2,1,0:T(1,128)S(1)}, u32[]{:S(2)}, u32[]{:S(2)}) collective-permute-start(f32[7,1,2048]{2,1,0:T(1,128)S(1)} %get-tuple-element.6), channel_id=1, source_target_pairs={{16,0},{32,16},{48,32},{64,48},{80,64},{96,80},{112,96},{128,112},... | collective-permute-start | bytes 172040 | tf_op jit(solution)/shard_map/ppermute | solution.py:22
  69.0 3.6 %all-to-all-done = f32[16,48,128]{2,0,1:T(8,128)S(1)} async-done(((f32[16,48,128]{2,0,1:T(8,128)}), f32[16,48,128]{2,0,1:T(8,128)S(1)}, u32[]{:S(2)}, u32[]{:S(2)}) %all-to-all-start) | async-done | bytes 393248 | tf_op jit(solution)/shard_map/all_to_all | solution.py:75
  74.4 56.3 %reduce-scatter.2.cloned.1.call-done = f32[16,3,128]{2,0,1:T(8,128)} async-done(((f32[256,3,128]{2,0,1:T(8,128)}), f32[16,3,128]{2,0,1:T(8,128)}) %reduce-scatter.2.cloned.1.call-update) | async-done | bytes 24592 | tf_op jit(solution)/shard_map/reduce_scatter | solution.py:80
  132.1 19.3 %all-to-all-start.1 = ((f32[16,3,128]{2,1,0:T(4,128)}), f32[16,3,128]{2,1,0:T(4,128)S(1)}, u32[]{:S(2)}, u32[]{:S(2)}) async-start(f32[16,3,128]{2,1,0:T(4,128)} %copy.50), calls=%async_computation.2 | async-start | bytes 65536 | tf_op jit(solution)/shard_map/all_to_all | solution.py:81
  151.3 7.3 %all-to-all-done.1 = f32[16,3,128]{2,1,0:T(4,128)S(1)} async-done(((f32[16,3,128]{2,1,0:T(4,128)}), f32[16,3,128]{2,1,0:T(4,128)S(1)}, u32[]{:S(2)}, u32[]{:S(2)}) %all-to-all-start.1) | async-done | bytes 24608 | tf_op jit(solution)/shard_map/all_to_all | solution.py:81
  159.9 3.7 %all-to-all-start.2 = ((f32[48,8,128]{2,1,0:T(8,128)}), f32[48,8,128]{2,1,0:T(8,128)S(1)}, u32[]{:S(2)}, u32[]{:S(2)}) async-start(f32[48,8,128]{2,1,0:T(8,128)} %multiply_multiply_fusion), calls=%async_computation.3 | async-start | bytes 393216 | tf_op jit(solution)/shard_map/all_to_all | solution.py:93
  163.7 8.1 %all-to-all-done.2 = f32[48,8,128]{2,1,0:T(8,128)S(1)} async-done(((f32[48,8,128]{2,1,0:T(8,128)}), f32[48,8,128]{2,1,0:T(8,128)S(1)}, u32[]{:S(2)}, u32[]{:S(2)}) %all-to-all-start.2) | async-done | bytes 196640 | tf_op jit(solution)/shard_map/all_to_all | solution.py:93
  174.6 2.6 %collective-permute-done.3 = f32[3,1,2048]{2,1,0:T(1,128)S(1)} collective-permute-done((f32[3,1,2048]{2,1,0:T(1,128)S(1)}, f32[3,1,2048]{2,1,0:T(1,128)S(1)}, u32[]{:S(2)}, u32[]{:S(2)}) %collective-permute-start.3) | collective-permute-done | bytes 24608 | tf_op jit(solution)/shard_map/ppermute | solution.py:19
  180.6 2.2 collective-permute-done.5
  186.3 2.4 %collective-permute-done.7 = f32[3,1,2048]{2,1,0:T(1,128)S(1)} collective-permute-done((f32[3,1,2048]{2,1,0:T(1,128)S(1)}, f32[3,1,2048]{2,1,0:T(1,128)S(1)}, u32[]{:S(2)}, u32[]{:S(2)}) %collective-permute-start.7) | collective-permute-done | bytes 24608 | tf_op jit(solution)/shard_map/ppermute | solution.py:19
  190.9 1.5 collective-permute-done.8
  192.4 1.9 collective-permute-done.9
  195.0 3.0 %copy.55 = f32[3,8,2048]{1,0,2:T(4,128)} copy(f32[3,8,2048]{2,1,0:T(8,128)S(1)} %fusion.13) | data formatting | bytes 393216 | tf_op jit(solution)/shard_map/add | solution.py:32
  198.0 4.4 %reshape.39 = f32[16,1,3072]{2,1,0:T(1,128)S(1)} reshape(f32[2048,3,8]{2,1,0:T(4,128)} %bitcast.57) | data formatting | bytes 393216
  202.5 16.5 %all_to_all.75 = f32[16,1,3072]{2,1,0:T(1,128)S(1)} all-to-all(f32[16,1,3072]{2,1,0:T(1,128)S(1)} %reshape.39), channel_id=1, replica_groups=mesh['gx'=16,'gy'=16] {'gy'}, dimensions={0} | all-to-all | bytes 393216 | tf_op jit(solution)/shard_map/all_to_all | solution.py:103
  220.6 4.1 %reshape.40 = f32[2048,3,8]{2,1,0:T(4,128)} reshape(f32[16,3072]{1,0:T(8,128)S(1)} %reduce) | data formatting | bytes 393216
  224.7 3.3 %copy.56 = f32[3,8,16,128]{3,1,0,2:T(8,128)S(1)} copy(f32[3,8,16,128]{1,0,3,2:T(4,128)} %bitcast.58) | data formatting | bytes 393216 | tf_op jit(solution)/shard_map/all_to_all | solution.py:103
  (65 shorter events, 24.6 us)
Async XLA Ops:
  6.5 152.1 %copy-start = (f32[48,48]{1,0:T(8,128)S(1)}, f32[48,48]{1,0:T(8,128)}, u32[]{:S(2)}) copy-start(f32[48,48]{1,0:T(8,128)} %param.19) | copy-start | bytes 27652
  8.3 49.9 %all-to-all-start.3 = ((f32[2,48,8,128]{3,2,0,1:T(8,128)}), f32[2,48,8,128]{3,2,0,1:T(8,128)S(1)}, u32[]{:S(2)}, u32[]{:S(2)}) async-start(f32[2,48,8,128]{3,2,0,1:T(8,128)} %pad_maximum_fusion), calls=%async_computation.4 | async-start | bytes 786432 | tf_op jit(solution)/shard_map/all_to_all | solution.py:89
  58.3 14.3 %all-to-all-start = ((f32[16,48,128]{2,0,1:T(8,128)}), f32[16,48,128]{2,0,1:T(8,128)S(1)}, u32[]{:S(2)}, u32[]{:S(2)}) async-start(f32[16,48,128]{2,0,1:T(8,128)} %copy.48), calls=%async_computation | async-start | bytes 786432 | tf_op jit(solution)/shard_map/all_to_all | solution.py:75
  62.7 68.0 %reduce-scatter.2.cloned.1.call-start = ((), (), s32[]{:S(2)}) async-start(), calls=%async_computation.6 | async-start | bytes 417792 | tf_op jit(solution)/shard_map/reduce_scatter | solution.py:80
  62.9 96.3 %copy-start.1 = (f32[48,8,128]{2,1,0:T(8,128)S(1)}, f32[48,8,128]{2,1,0:T(8,128)}, u32[]{:S(2)}) copy-start(f32[48,8,128]{2,1,0:T(8,128)} %param.17) | copy-start | bytes 589828
  63.1 10.7 %collective-permute-start = (f32[7,1,2048]{2,1,0:T(1,128)S(1)}, f32[7,1,2048]{2,1,0:T(1,128)S(1)}, u32[]{:S(2)}, u32[]{:S(2)}) collective-permute-start(f32[7,1,2048]{2,1,0:T(1,128)S(1)} %get-tuple-element.5), channel_id=1, source_target_pairs={{0,16},{16,32},{32,48},{48,64},{64,80},{80,96},{96,112},{112,128},... | collective-permute-start | bytes 172040 | tf_op jit(solution)/shard_map/ppermute | solution.py:19
  64.8 9.0 %collective-permute-start.1 = (f32[7,1,2048]{2,1,0:T(1,128)S(1)}, f32[7,1,2048]{2,1,0:T(1,128)S(1)}, u32[]{:S(2)}, u32[]{:S(2)}) collective-permute-start(f32[7,1,2048]{2,1,0:T(1,128)S(1)} %get-tuple-element.6), channel_id=1, source_target_pairs={{16,0},{32,16},{48,32},{64,48},{80,64},{96,80},{112,96},{128,112},... | collective-permute-start | bytes 172040 | tf_op jit(solution)/shard_map/ppermute | solution.py:22
  132.1 26.6 %all-to-all-start.1 = ((f32[16,3,128]{2,1,0:T(4,128)}), f32[16,3,128]{2,1,0:T(4,128)S(1)}, u32[]{:S(2)}, u32[]{:S(2)}) async-start(f32[16,3,128]{2,1,0:T(4,128)} %copy.50), calls=%async_computation.2 | async-start | bytes 65536 | tf_op jit(solution)/shard_map/all_to_all | solution.py:81
  159.9 11.9 %all-to-all-start.2 = ((f32[48,8,128]{2,1,0:T(8,128)}), f32[48,8,128]{2,1,0:T(8,128)S(1)}, u32[]{:S(2)}, u32[]{:S(2)}) async-start(f32[48,8,128]{2,1,0:T(8,128)} %multiply_multiply_fusion), calls=%async_computation.3 | async-start | bytes 393216 | tf_op jit(solution)/shard_map/all_to_all | solution.py:93
  171.9 2.8 %collective-permute-start.2 = (f32[3,1,2048]{2,1,0:T(1,128)S(1)}, f32[3,1,2048]{2,1,0:T(1,128)S(1)}, u32[]{:S(2)}, u32[]{:S(2)}) collective-permute-start(f32[3,1,2048]{2,1,0:T(1,128)S(1)} %get-tuple-element.16), channel_id=1, source_target_pairs={{16,0},{32,16},{48,32},{64,48},{80,64},{96,80},{112,96},{128,112},... | collective-permute-start | bytes 73736 | tf_op jit(solution)/shard_map/ppermute | solution.py:22
  172.4 4.8 %collective-permute-start.3 = (f32[3,1,2048]{2,1,0:T(1,128)S(1)}, f32[3,1,2048]{2,1,0:T(1,128)S(1)}, u32[]{:S(2)}, u32[]{:S(2)}) collective-permute-start(f32[3,1,2048]{2,1,0:T(1,128)S(1)} %get-tuple-element.15), channel_id=1, source_target_pairs={{0,16},{16,32},{32,48},{48,64},{64,80},{80,96},{96,112},{112,128},... | collective-permute-start | bytes 73736 | tf_op jit(solution)/shard_map/ppermute | solution.py:19
  177.9 2.8 %collective-permute-start.4 = (f32[3,1,2048]{2,1,0:T(1,128)S(1)}, f32[3,1,2048]{2,1,0:T(1,128)S(1)}, u32[]{:S(2)}, u32[]{:S(2)}) collective-permute-start(f32[3,1,2048]{2,1,0:T(1,128)S(1)} %get-tuple-element.14), channel_id=1, source_target_pairs={{16,0},{32,16},{48,32},{64,48},{80,64},{96,80},{112,96},{128,112},... | collective-permute-start | bytes 73736 | tf_op jit(solution)/shard_map/ppermute | solution.py:22
  178.0 4.9 %collective-permute-start.5 = (f32[3,1,2048]{2,1,0:T(1,128)S(1)}, f32[3,1,2048]{2,1,0:T(1,128)S(1)}, u32[]{:S(2)}, u32[]{:S(2)}) collective-permute-start(f32[3,1,2048]{2,1,0:T(1,128)S(1)} %get-tuple-element.13), channel_id=1, source_target_pairs={{0,16},{16,32},{32,48},{48,64},{64,80},{80,96},{96,112},{112,128},... | collective-permute-start | bytes 73736 | tf_op jit(solution)/shard_map/ppermute | solution.py:19
  183.5 2.8 %collective-permute-start.6 = (f32[3,1,2048]{2,1,0:T(1,128)S(1)}, f32[3,1,2048]{2,1,0:T(1,128)S(1)}, u32[]{:S(2)}, u32[]{:S(2)}) collective-permute-start(f32[3,1,2048]{2,1,0:T(1,128)S(1)} %get-tuple-element.12), channel_id=1, source_target_pairs={{16,0},{32,16},{48,32},{64,48},{80,64},{96,80},{112,96},{128,112},... | collective-permute-start | bytes 73736 | tf_op jit(solution)/shard_map/ppermute | solution.py:22
  183.6 5.0 %collective-permute-start.7 = (f32[3,1,2048]{2,1,0:T(1,128)S(1)}, f32[3,1,2048]{2,1,0:T(1,128)S(1)}, u32[]{:S(2)}, u32[]{:S(2)}) collective-permute-start(f32[3,1,2048]{2,1,0:T(1,128)S(1)} %get-tuple-element.11), channel_id=1, source_target_pairs={{0,16},{16,32},{32,48},{48,64},{64,80},{80,96},{96,112},{112,128},... | collective-permute-start | bytes 73736 | tf_op jit(solution)/shard_map/ppermute | solution.py:19
  189.4 3.0 %collective-permute-start.8 = (f32[3,1,2048]{2,1,0:T(1,128)S(1)}, f32[3,1,2048]{2,1,0:T(1,128)S(1)}, u32[]{:S(2)}, u32[]{:S(2)}) collective-permute-start(f32[3,1,2048]{2,1,0:T(1,128)S(1)} %get-tuple-element.10), channel_id=1, source_target_pairs={{16,0},{32,16},{48,32},{64,48},{80,64},{96,80},{112,96},{128,112},... | collective-permute-start | bytes 73736 | tf_op jit(solution)/shard_map/ppermute | solution.py:22
  189.5 4.9 %collective-permute-start.9 = (f32[3,1,2048]{2,1,0:T(1,128)S(1)}, f32[3,1,2048]{2,1,0:T(1,128)S(1)}, u32[]{:S(2)}, u32[]{:S(2)}) collective-permute-start(f32[3,1,2048]{2,1,0:T(1,128)S(1)} %get-tuple-element.9), channel_id=1, source_target_pairs={{0,16},{16,32},{32,48},{48,64},{64,80},{80,96},{96,112},{112,128},... | collective-permute-start | bytes 73736 | tf_op jit(solution)/shard_map/ppermute | solution.py:19
Sparse Core Ops, SparseCore 0:
  73.9 56.7 reduce-scatter.1

commit v2 on v1

v2 whole, which is shorter than its diff:
```python
import functools

import jax
import jax.numpy as jnp
from jax import lax
from jax.experimental import pallas as pl
from jax.experimental.pallas import tpu as pltpu
from jax.sharding import PartitionSpec as P

MESH = pl.DeviceIdType.MESH
F32 = jnp.float32
BF16 = jnp.bfloat16
LEV = 48
LANES = 128
PASSES = 4


def two_terms(x):
    high = x.astype(BF16)
    return high, (x - high.astype(F32)).astype(BF16)


def mul(a, b):
    return jnp.dot(a, b, preferred_element_type=F32)


def mul_terms(a, b):
    a_high, a_low = two_terms(a)
    b_high, b_low = two_terms(b)
    return mul(a_high, b_high) + mul(a_high, b_low) + mul(a_low, b_high)


def lane_of(shape):
    return lax.broadcasted_iota(jnp.int32, shape, len(shape) - 1)


def kernel(
    nz,
    ng,
    vals_hbm,
    weight,
    box,
    owner,
    count,
    dx_hbm,
    dy_hbm,
    sp_hbm,
    land,
    corr,
    out_hbm,
    vals,
    raw,
    ext,
    edge,
    pack_s,
    pack_r,
    slab_s,
    slab_r,
    sums_s,
    sums_r,
    own_s,
    own_r,
    part_s,
    part_r,
    tile_s,
    tile_r,
    box_s,
    box_r,
    field,
    out_v,
    local_sem,
    bulk_send,
    bulk_recv,
    pack_send,
    pack_recv,
    slab_send,
    slab_recv,
    all_send,
    all_recv,
    box_send,
    box_recv,
):
    group = 2 * ng
    per = LEV // ng
    rows1 = per * 8
    rows3 = tile_s.shape[0] // ng
    owners = nz * ng
    depth = group * 8
    gx = lax.axis_index("gx")
    gy = lax.axis_index("gy")
    half = lax.div(gx, nz)
    z = lax.rem(gx, nz)
    me = half * ng + gy

    def member(step):
        index = lax.rem(me + step, group)
        h = lax.div(index, ng)
        g = lax.rem(index, ng)
        return index, h, g, (h * nz + z, g)

    def along_z(step):
        target = lax.rem(z + step, nz)
        return target, (half * nz + target, gy)

    east = (lax.rem(gx + 1, 2 * nz), gy)
    west = (lax.rem(gx + 2 * nz - 1, 2 * nz), gy)
    north = (gx, lax.rem(gy + 1, ng))
    south = (gx, lax.rem(gy + ng - 1, ng))

    def remote(src, dst, send, recv, device):
        return pltpu.make_async_remote_copy(
            src_ref=src,
            dst_ref=dst,
            send_sem=send,
            recv_sem=recv,
            device_id=device,
            device_id_type=MESH,
        )

    loads = [
        pltpu.make_async_copy(dx_hbm, raw.at[0], local_sem.at[0]),
        pltpu.make_async_copy(dy_hbm, raw.at[1], local_sem.at[1]),
        pltpu.make_async_copy(sp_hbm, raw.at[2], local_sem.at[2]),
        pltpu.make_async_copy(vals_hbm, vals, local_sem.at[3]),
    ]
    for load in loads:
        load.start()

    barrier = pltpu.get_barrier_semaphore()

    def greet_plane(step, _):
        pl.semaphore_signal(barrier, inc=1, device_id=member(step)[3], device_id_type=MESH)
        return _

    def greet_z(step, _):
        pl.semaphore_signal(barrier, inc=1, device_id=along_z(step)[1], device_id_type=MESH)
        return _

    lax.fori_loop(1, group, greet_plane, 0)
    lax.fori_loop(1, nz, greet_z, 0)
    for device in (east, west):
        pl.semaphore_signal(barrier, inc=1, device_id=device, device_id_type=MESH)

    for load in loads[:3]:
        load.wait()
    mask = land[...].astype(F32)
    for x in range(8):
        for a in range(3):
            value = raw[a, pl.ds(x, LEV, stride=8), :]
            if a == 2:
                value = value * mask[x : x + 1, :]
            ext[4 + x, a] = value

    lane1 = lane_of((1, LANES))
    base = lax.rem(me * 8, LANES)
    for parity in range(2):
        row = jnp.zeros((1, LANES), jnp.int32)
        for j in range(8):
            row = jnp.where(lane1 == base + j, owner[2 * j + parity], row)
        own_s[parity : parity + 1, :] = row

    pl.semaphore_wait(barrier, group + nz)

    bulk = [
        remote(ext.at[pl.ds(4, 4)], ext.at[pl.ds(12, 4)], bulk_send.at[0], bulk_recv.at[0], west),
        remote(ext.at[pl.ds(8, 4)], ext.at[pl.ds(0, 4)], bulk_send.at[1], bulk_recv.at[1], east),
    ]
    for copy in bulk:
        copy.start()

    def send_owners(step, _):
        _, _, _, device = member(step)
        remote(own_s, own_r.at[me], all_send.at[0], all_recv.at[0], device).start()
        return _

    lax.fori_loop(1, group, send_owners, 0)
    own_r[me] = own_s[...]

    loads[3].wait()
    weighted = jnp.where(
        lax.broadcasted_iota(jnp.int32, (16, LANES), 0) < count[0], weight[...], 0.0
    )
    boxes = box[...]
    place = (boxes >> 6) * LANES + (boxes & 63)
    target = lax.broadcasted_iota(jnp.int32, (2 * LANES, LANES), 0)
    for j in range(8):
        terms = []
        hots = []
        for parity in range(2):
            b = 2 * j + parity
            value = vals[b].astype(F32) * weighted[b : b + 1, :]
            terms.append(two_terms(value))
            hit = target == place[b : b + 1, :] + 64 * parity
            hots.append(jnp.where(hit, 1.0, 0.0).astype(BF16))
        left = jnp.concatenate(
            [
                jnp.concatenate([terms[0][0], terms[1][0]], axis=1),
                jnp.concatenate([terms[0][1], terms[1][1]], axis=1),
            ],
            axis=0,
        )
        hot = jnp.concatenate(hots, axis=1)
        total = lax.dot_general(left, hot, (((1,), (1,)), ((), ())), preferred_element_type=F32)
        total = total[:LEV] + total[LEV:]
        sums_s[0, pl.ds(j, LEV, stride=8), :] = total[:, :LANES]
        sums_s[1, pl.ds(j, LEV, stride=8), :] = total[:, LANES:]

    def rows_of(g):
        return pl.ds(pl.multiple_of(g * rows1, 8), rows1)

    def send_sums(step, _):
        _, h, g, device = member(step)
        remote(
            sums_s.at[h, rows_of(g)], sums_r.at[me], all_send.at[1], all_recv.at[1], device
        ).start()
        return _

    lax.fori_loop(1, group, send_sums, 0)
    sums_r[me] = sums_s[half, rows_of(gy), :]

    lane = lane_of((LEV, LANES))
    for part in range(2):
        to_south = jnp.zeros((LEV, LANES), F32)
        to_north = jnp.zeros((LEV, LANES), F32)
        for r in range(4):
            for a in range(3):
                q = 3 * r + a
                value = ext[4 + 4 * part + r, a]
                if q:
                    value = pltpu.roll(value, 8 * q, 1)
                low = (8 * q + LANES - 4) % LANES
                to_south = jnp.where((lane >= 8 * q) & (lane < 8 * q + 4), value, to_south)
                to_north = jnp.where((lane >= low) & (lane < low + 4), value, to_north)
        pack_s[0, part] = to_south
        pack_s[1, part] = to_north
    packs = [
        remote(pack_s.at[0], pack_r.at[0], pack_send.at[0], pack_recv.at[0], south),
        remote(pack_s.at[1], pack_r.at[1], pack_send.at[1], pack_recv.at[1], north),
    ]
    for copy in packs:
        copy.start()

    level = lax.broadcasted_iota(jnp.int32, (LEV, ng * rows3), 0)
    column = lane_of((LEV, ng * rows3))
    from_group = column // rows3
    within = column - from_group * rows3
    own_level = (within < per) & (from_group * per + within == level)
    near_level = (
        (within >= per) & (within < 2 * per) & (from_group * per + within - per == level)
    )
    corr_v = corr[...]
    corr_rows = jnp.concatenate(
        [
            jnp.dot(
                corr_v,
                jnp.where(chosen, 1.0, 0.0),
                precision=lax.Precision.HIGHEST,
                preferred_element_type=F32,
            )
            for chosen in (own_level, near_level)
        ],
        axis=0,
    )

    for copy in packs:
        copy.wait()
    for part in range(2):
        from_north = jnp.where(gy < ng - 1, pack_r[0, part], 0.0)
        from_south = jnp.where(gy > 0, pack_r[1, part], 0.0)
        slab_s[part] = jnp.where((lane & 7) < 4, from_north, from_south)
    slabs = [
        remote(slab_s.at[0], slab_r.at[1], slab_send.at[0], slab_recv.at[0], west),
        remote(slab_s.at[1], slab_r.at[0], slab_send.at[1], slab_recv.at[1], east),
    ]
    for copy in slabs:
        copy.start()

    def wait_bytes(ref, sem, size):
        view = ref.at[pl.ds(0, size)]
        pltpu.make_async_copy(view, view, sem).wait()

    wait_bytes(own_r, all_recv.at[0], group - 1)
    wide = (depth + LANES - 1) // LANES
    owner_rows = []
    for parity in range(2):
        pieces = []
        for piece in range(wide):
            row = jnp.zeros((1, LANES), jnp.int32)
            for source in range(piece * 16, min(group, piece * 16 + 16)):
                row = row + own_r[source, parity : parity + 1, :]
            pieces.append(row)
        row = jnp.concatenate(pieces, axis=1) if wide > 1 else pieces[0]
        owner_rows.append(row[:, :depth])
    candidate = lax.broadcasted_iota(jnp.int32, (owners, depth), 0)
    hits = jnp.concatenate(
        [
            jnp.where(owner_rows[parity] == candidate + shift, 1.0, 0.0).astype(BF16)
            for parity, shift in ((0, 0), (1, 0), (1, owners), (0, owners))
        ],
        axis=1,
    )
    wait_bytes(sums_r, all_recv.at[1], group - 1)
    lower = lane_of((depth, LANES)) < 64
    columns = []
    for t in range(per):
        value = sums_r[:, t * 8 : t * 8 + 8, :].reshape(depth, LANES)
        other = pltpu.roll(value, 64, 1)
        columns.append(
            jnp.concatenate(
                [
                    jnp.where(lower, value, 0.0),
                    jnp.where(lower, other, 0.0),
                    jnp.where(lower, 0.0, value),
                    jnp.where(lower, 0.0, other),
                ],
                axis=0,
            )
        )
    stack_high, stack_low = two_terms(jnp.concatenate(columns, axis=1))
    by_owner = mul(hits, stack_high) + mul(hits, stack_low)
    for t in range(per):
        part_s[:, t] = by_owner[:, t * LANES : (t + 1) * LANES].reshape(nz, ng, LANES)

    def send_parts(step, _):
        index, device = along_z(step)
        remote(
            part_s.at[index], part_r.at[z], all_send.at[2], all_recv.at[2], device
        ).start()
        return _

    lax.fori_loop(1, nz, send_parts, 0)
    part_r[z] = part_s[z]

    for copy in slabs:
        copy.wait()
    outer = (lane < 4) | (lane >= LANES - 4)
    for part in range(4):
        slab = (slab_r[0], slab_s[0], slab_s[1], slab_r[1])[part]
        for r in range(4):
            for a in range(3):
                q = 3 * r + a
                value = pltpu.roll(slab, LANES - 8 * q, 1) if q else slab
                edge[4 * part + r, a] = jnp.where(outer, value, 0.0)
    for copy in bulk:
        copy.wait()

    def faces(x, _):
        here, beyond = ext[x, 2], edge[x, 2]
        last = lane == LANES - 1
        turned, turned_beyond = pltpu.roll(here, LANES - 1, 1), pltpu.roll(beyond, LANES - 1, 1)
        ext[x, 0] = jnp.where(here * ext[x + 1, 2] > 0.0, ext[x, 0], 0.0)
        edge[x, 0] = jnp.where(beyond * edge[x + 1, 2] > 0.0, edge[x, 0], 0.0)
        upper = jnp.where(last, turned_beyond, turned)
        upper_beyond = jnp.where(last, turned, turned_beyond)
        ext[x, 1] = jnp.where(here * upper > 0.0, ext[x, 1], 0.0)
        edge[x, 1] = jnp.where(beyond * upper_beyond > 0.0, edge[x, 1], 0.0)
        return _

    lax.fori_loop(0, 15, faces, 0)

    wait_bytes(part_r, all_recv.at[2], nz - 1)
    tile_s[...] = jnp.zeros(tile_s.shape, F32)
    row = lax.broadcasted_iota(jnp.int32, (ng, LANES), 0)
    box_column = lane_of((ng, LANES)) & 15
    for t in range(per):
        value = part_r[0, t]
        for source in range(1, nz):
            value = value + part_r[source, t]
        below = jnp.where(row == 0, 0.0, pltpu.roll(value, 1, 0))
        above = jnp.where(row == ng - 1, 0.0, pltpu.roll(value, ng - 1, 0))
        tile_s[pl.ds(t, ng, stride=rows3), :] = value
        tile_s[pl.ds(per + t, ng, stride=rows3), :] = jnp.where(box_column == 15, below, above)

    def tile_rows(g):
        return pl.ds(pl.multiple_of(g * rows3, 8), rows3)

    def send_tiles(step, _):
        _, _, g, device = member(step)
        remote(
            tile_s.at[tile_rows(g)], tile_r.at[me], all_send.at[3], all_recv.at[3], device
        ).start()
        return _

    lax.fori_loop(1, group, send_tiles, 0)
    tile_r[me] = tile_s[tile_rows(gy), :]

    wait_bytes(tile_r, all_recv.at[3], group - 1)
    arrived = jnp.concatenate(
        [tile_r[h * ng : (h + 1) * ng].reshape(ng * rows3, LANES) for h in range(2)], axis=1
    )
    mixed = mul_terms(corr_rows, arrived)
    for h in range(2):
        mine = mixed[:LEV, h * LANES : (h + 1) * LANES]
        near = mixed[LEV:, h * LANES : (h + 1) * LANES]
        turned = pltpu.roll(jnp.where(half == 0, near, mine), 64, 1)
        low_part = jnp.where(half == 0, mine, turned)
        high_part = jnp.where(half == 0, turned, near)
        box_s[h] = jnp.where(lane < 64, low_part, high_part)
    borders = [
        remote(box_s.at[0], box_r.at[1], box_send.at[0], box_recv.at[0], west),
        remote(box_s.at[1], box_r.at[0], box_send.at[1], box_recv.at[1], east),
    ]
    for copy in borders:
        copy.start()
    for copy in borders:
        copy.wait()

    lane8 = lane_of((8, LANES))
    first, last = lane8 == 0, lane8 == LANES - 1

    def advance(step, _):
        rows = pl.ds(pl.multiple_of(step * 8, 8), 8)
        inner, outside = [], []
        for part in range(4):
            source = (box_r.at[0], box_s.at[0], box_s.at[1], box_r.at[1])[part]
            value = source[rows, :]
            for r in range(4):
                x = 4 * part + r
                at_inner = 16 * r + (lane8 >> 3)
                at_outside = jnp.where(lane8 < 64, 64 + 16 * r, 64 + 16 * r + 15)
                inner.append(ext[x, 2, rows, :] * jnp.take_along_axis(value, at_inner, axis=1))
                outside.append(
                    edge[x, 2, rows, :] * jnp.take_along_axis(value, at_outside, axis=1)
                )
        for turn in range(PASSES):
            low, high = 1 + turn, 15 - turn
            flow = {}
            for x in range(low - 1, high):
                flow[x] = (
                    ext[x, 0, rows, :] * (inner[x + 1] - inner[x]),
                    edge[x, 0, rows, :] * (outside[x + 1] - outside[x]),
                )
            new_inner, new_outside = list(inner), list(outside)
            for x in range(low, high):
                here, beyond = inner[x], outside[x]
                turned = pltpu.roll(here, LANES - 1, 1)
                turned_beyond = pltpu.roll(beyond, LANES - 1, 1)
                up = ext[x, 1, rows, :] * (jnp.where(last, turned_beyond, turned) - here)
                up_beyond = edge[x, 1, rows, :] * (
                    jnp.where(last, turned, turned_beyond) - beyond
                )
                back, back_beyond = pltpu.roll(up, 1, 1), pltpu.roll(up_beyond, 1, 1)
                down = jnp.where(first, back_beyond, back)
                down_beyond = jnp.where(first, back, back_beyond)
                new_inner[x] = here + (flow[x][0] - flow[x - 1][0]) + (up - down)
                new_outside[x] = beyond + (flow[x][1] - flow[x - 1][1]) + (up_beyond - down_beyond)
            inner, outside = new_inner, new_outside
        for x in range(8):
            field[x, rows, :] = inner[4 + x]
        return _

    lax.fori_loop(0, LEV // 8, advance, 0)

    whole = jnp.concatenate([field[x] for x in range(8)], axis=1)
    result = mul_terms(corr_v, whole)
    for x in range(8):
        out_v[pl.ds(x, LEV, stride=8), :] = ext[4 + x, 2] * result[:, x * LANES : (x + 1) * LANES]
    store = pltpu.make_async_copy(out_v, out_hbm, local_sem.at[4])
    store.start()

    def wait_sent(ref, sem, size):
        view = ref.at[pl.ds(0, size)]
        pltpu.make_async_copy(view, view, sem).wait()

    wait_sent(own_r, all_send.at[0], group - 1)
    wait_sent(sums_r, all_send.at[1], group - 1)
    wait_sent(part_r, all_send.at[2], nz - 1)
    wait_sent(tile_r, all_send.at[3], group - 1)
    store.wait()


def local(
    nz,
    ng,
    obs_values,
    obs_weight,
    obs_box,
    obs_owner,
    block_count,
    diff_x,
    diff_y,
    spread_std,
    land_sea,
    vert_corr,
):
    group = 2 * ng
    per = LEV // ng
    rows3 = -(-2 * per // 8) * 8
    vmem = pl.BlockSpec(memory_space=pltpu.VMEM)
    smem = pl.BlockSpec(memory_space=pltpu.SMEM)
    hbm = pl.BlockSpec(memory_space=pl.ANY)
    dma = pltpu.SemaphoreType.DMA
    flat = (LEV * 8, LANES)
    out = pl.pallas_call(
        functools.partial(kernel, nz, ng),
        out_shape=jax.ShapeDtypeStruct(flat, F32),
        in_specs=[hbm, vmem, vmem, smem, smem, hbm, hbm, hbm, vmem, vmem],
        out_specs=hbm,
        scratch_shapes=[
            pltpu.VMEM((16, LEV, LANES), BF16),
            pltpu.VMEM((3,) + flat, F32),
            pltpu.VMEM((16, 3, LEV, LANES), F32),
            pltpu.VMEM((16, 3, LEV, LANES), F32),
            pltpu.VMEM((2, 2, LEV, LANES), F32),
            pltpu.VMEM((2, 2, LEV, LANES), F32),
            pltpu.VMEM((2, LEV, LANES), F32),
            pltpu.VMEM((2, LEV, LANES), F32),
            pltpu.VMEM((2,) + flat, F32),
            pltpu.VMEM((group, per * 8, LANES), F32),
            pltpu.VMEM((2, LANES), jnp.int32),
            pltpu.VMEM((group, 2, LANES), jnp.int32),
            pltpu.VMEM((nz, per, ng, LANES), F32),
            pltpu.VMEM((nz, per, ng, LANES), F32),
            pltpu.VMEM((ng * rows3, LANES), F32),
            pltpu.VMEM((group, rows3, LANES), F32),
            pltpu.VMEM((2, LEV, LANES), F32),
            pltpu.VMEM((2, LEV, LANES), F32),
            pltpu.VMEM((8, LEV, LANES), F32),
            pltpu.VMEM(flat, F32),
            dma((5,)),
            dma((2,)),
            dma((2,)),
            dma((2,)),
            dma((2,)),
            dma((2,)),
            dma((2,)),
            dma((4,)),
            dma((4,)),
            dma((2,)),
            dma((2,)),
        ],
        compiler_params=pltpu.CompilerParams(
            collective_id=0, has_side_effects=True, vmem_limit_bytes=40 * 1024 * 1024
        ),
        name="analysis",
    )(
        obs_values,
        obs_weight,
        obs_box,
        obs_owner,
        block_count,
        diff_x.reshape(flat),
        diff_y.reshape(flat),
        spread_std.reshape(flat),
        land_sea,
        vert_corr,
    )
    return out.reshape(LEV, 8, LANES)


def solution(mesh):
    in_specs = (
        P(("gx", "gy"), None, None),
        P(("gx", "gy"), None),
        P(("gx", "gy"), None),
        P(("gx", "gy")),
        P(("gx", "gy")),
        P(None, "gx", "gy"),
        P(None, "gx", "gy"),
        P(None, "gx", "gy"),
        P("gx", "gy"),
        P(),
    )
    return jax.shard_map(
        functools.partial(local, mesh.shape["gx"] // 2, mesh.shape["gy"]),
        mesh=mesh,
        in_specs=in_specs,
        out_specs=P(None, "gx", "gy"),
        check_vma=False,
    )
```

time: 237 us -> 52.5 us (0.22)
  waiting for transfers between devices: 89.4 us -> 0 us
  blocking collectives: 50.5 us -> 0 us
  starting transfers between devices: 47.9 us -> 0 us
  Pallas kernels: 0 us -> 44.3 us
  between operations: 15 us -> 0.69 us
  local copies, waits for them, and re-layouts: 20.5 us -> 7.16 us
  other arithmetic: 9.19 us -> 0 us
  matrix products: 3.35 us -> 0 us
    reduce_scatter x1 -> x0, waiting for transfers between devices: 56.3 us -> none  [local(): mine = lax.psum_scatter(partial, 'gx', scatter_dimension=0, tiled=True)]
    pallas_call x0 -> x1, Pallas kernels: none -> 44.3 us  [local(): pl.pallas_call(functools.partial(kernel, nz, ng), out_shape=jax.ShapeDtyp...]
    all_to_all x4 -> x0, starting transfers between devices: 35.8 us -> none  [the longest x1 19.3 us: local(): lax.all_to_all(mine, 'gy', split_axis=0, concat_axis=1, tiled=True)[0]]
    all_gather x1 -> x0, blocking collectives: 22.7 us -> none  [local(): mask_whole = lax.all_gather(mask, 'gy', axis=1, tiled=True)]
    all_to_all x4 -> x0, waiting for transfers between devices: 19 us -> none  [the longest x1 8.12 us: local(): lax.all_to_all(forcing, 'gy', split_axis=0, concat_axis=2, tiled=True)]
    all_to_all x1 -> x0, blocking collectives: 16.5 us -> none  [local(): field = lax.all_to_all(field, 'gy', split_axis=2, concat_axis=0, tiled=True)]
    ppermute x10 -> x0, waiting for transfers between devices: 14.2 us -> none  [the longest x5 9.05 us: extended(): lax.ppermute(lax.slice_in_dim(block, block.shape[dim] - width, None, axis...]
    ppermute x10 -> x0, starting transfers between devices: 12 us -> none  [the longest x5 7.11 us: extended(): lax.ppermute(lax.slice_in_dim(block, block.shape[dim] - width, None, axis...]
  transfers between devices with their start and end apart: 15 -> 0, of which waited for: 12 -> 0; matrix products, arithmetic and copies ran while one was open for 4% -> 0% of each run, Pallas kernels for 0% -> 0%
where the time goes in v2:
time: 52.5 us; the launch traced here: 52.1 us
  Pallas kernels  44.3 us (84%)
  local copies, waits for them, and re-layouts  7.16 us (14%)
  between operations  0.69 us (1%)
    pallas_call x1, Pallas kernels, local(): pl.pallas_call(functools.partial(kernel, nz, ng), out_shape=jax.ShapeDtyp...  44.3 us
    unnamed x19, local copies, waits for them, and re-layouts  7.16 us

profile of v2, /device:TPU:1, one launch (start us, length us, event | category | flops | bytes accessed | tf_op | source)
XLA Modules:
  0.0 52.1 jit_solution(6555407293828774329)
XLA Ops:
  0.0 0.0 copy-start.7
  0.7 0.0 copy-start.8
  0.7 0.0 copy-done.7
  0.7 0.6 %copy-done.8 = s32[16]{0:T(128)S(1)} copy-done((s32[16]{0:T(128)S(1)}, s32[16]{0:T(128)}, u32[]{:S(2)}) %copy-start.8) | copy-done | bytes 88
  1.3 0.0 copy-start
  1.3 0.9 %copy-done = bf16[16,48,128]{2,1,0:T(8,128)(2,1)S(1)} copy-done((bf16[16,48,128]{2,1,0:T(8,128)(2,1)S(1)}, bf16[16,48,128]{2,1,0:T(8,128)(2,1)}, u32[]{:S(2)}) %copy-start) | copy-done | bytes 196632
  2.3 0.0 copy-start.1
  2.3 0.9 %copy-done.1 = f32[48,8,128]{2,1,0:T(8,128)S(1)} copy-done((f32[48,8,128]{2,1,0:T(8,128)S(1)}, f32[48,8,128]{2,1,0:T(8,128)}, u32[]{:S(2)}) %copy-start.1) | copy-done | bytes 196632
  3.2 0.0 copy-start.2
  3.2 0.9 %copy-done.2 = f32[48,8,128]{2,1,0:T(8,128)S(1)} copy-done((f32[48,8,128]{2,1,0:T(8,128)S(1)}, f32[48,8,128]{2,1,0:T(8,128)}, u32[]{:S(2)}) %copy-start.2) | copy-done | bytes 196632
  4.1 0.0 copy-start.3
  4.1 0.9 %copy-done.3 = f32[48,8,128]{2,1,0:T(8,128)S(1)} copy-done((f32[48,8,128]{2,1,0:T(8,128)S(1)}, f32[48,8,128]{2,1,0:T(8,128)}, u32[]{:S(2)}) %copy-start.3) | copy-done | bytes 196632
  5.0 0.0 copy-start.4
  5.0 0.7 %copy-done.4 = f32[48,48]{1,0:T(8,128)S(1)} copy-done((f32[48,48]{1,0:T(8,128)S(1)}, f32[48,48]{1,0:T(8,128)}, u32[]{:S(2)}) %copy-start.4) | copy-done | bytes 9240
  5.8 0.0 copy-start.5
  5.8 0.7 %copy-done.5 = f32[16,128]{1,0:T(8,128)S(1)} copy-done((f32[16,128]{1,0:T(8,128)S(1)}, f32[16,128]{1,0:T(8,128)}, u32[]{:S(2)}) %copy-start.5) | copy-done | bytes 8216
  6.5 0.0 copy-start.6
  6.5 0.7 %copy-done.6 = s32[16,128]{1,0:T(8,128)S(1)} copy-done((s32[16,128]{1,0:T(8,128)S(1)}, s32[16,128]{1,0:T(8,128)}, u32[]{:S(2)}) %copy-start.6) | copy-done | bytes 8216
  7.2 44.3 %analysis.1 = f32[384,128]{1,0:T(8,128)S(1)} custom-call(bf16[16,48,128]{2,1,0:T(8,128)(2,1)S(1)} %copy-done, f32[16,128]{1,0:T(8,128)S(1)} %copy-done.5, s32[16,128]{1,0:T(8,128)S(1)} %copy-done.6, s32[16]{0:T(128)S(1)} %copy-done.8, s32[1]{0:T(128)S(6)} %copy.12.count, f32[384,128]{1,0:T(8,128)S(1)} %bitcast.5, f32[384,128]{1,0:T(8,128)S(1)} %bitcast.6, ...), custom_call_target="tpu_custom_call" | custom-call | tf_op jit(solution)/shard_map/analysis/pallas_call | solution.py:494
  51.5 0.7 %copy.13 = f32[48,8,128]{2,1,0:T(8,128)} copy(f32[48,8,128]{2,1,0:T(8,128)S(1)} %bitcast.4) | data formatting | bytes 393216
Async XLA Ops:
  0.0 0.7 %copy-start.7 = (s32[8,128]{1,0:T(8,128)S(1)}, s32[8,128]{1,0:T(8,128)}, u32[]{:S(2)}) copy-start(s32[8,128]{1,0:T(8,128)} %land.1) | copy-start | bytes 12292
  0.7 0.7 %copy-start.8 = (s32[16]{0:T(128)S(1)}, s32[16]{0:T(128)}, u32[]{:S(2)}) copy-start(s32[16]{0:T(128)} %owner.1) | copy-start | bytes 196
  1.3 0.9 %copy-start = (bf16[16,48,128]{2,1,0:T(8,128)(2,1)S(1)}, bf16[16,48,128]{2,1,0:T(8,128)(2,1)}, u32[]{:S(2)}) copy-start(bf16[16,48,128]{2,1,0:T(8,128)(2,1)} %vals_hbm.1) | copy-start | bytes 589828
  2.3 0.9 %copy-start.1 = (f32[48,8,128]{2,1,0:T(8,128)S(1)}, f32[48,8,128]{2,1,0:T(8,128)}, u32[]{:S(2)}) copy-start(f32[48,8,128]{2,1,0:T(8,128)} %param.15) | copy-start | bytes 589828
  3.2 0.9 %copy-start.2 = (f32[48,8,128]{2,1,0:T(8,128)S(1)}, f32[48,8,128]{2,1,0:T(8,128)}, u32[]{:S(2)}) copy-start(f32[48,8,128]{2,1,0:T(8,128)} %param.16) | copy-start | bytes 589828
  4.1 0.9 %copy-start.3 = (f32[48,8,128]{2,1,0:T(8,128)S(1)}, f32[48,8,128]{2,1,0:T(8,128)}, u32[]{:S(2)}) copy-start(f32[48,8,128]{2,1,0:T(8,128)} %param.17) | copy-start | bytes 589828
  5.0 0.7 %copy-start.4 = (f32[48,48]{1,0:T(8,128)S(1)}, f32[48,48]{1,0:T(8,128)}, u32[]{:S(2)}) copy-start(f32[48,48]{1,0:T(8,128)} %corr.1) | copy-start | bytes 27652
  5.8 0.7 %copy-start.5 = (f32[16,128]{1,0:T(8,128)S(1)}, f32[16,128]{1,0:T(8,128)}, u32[]{:S(2)}) copy-start(f32[16,128]{1,0:T(8,128)} %weight.1) | copy-start | bytes 24580
  6.5 0.7 %copy-start.6 = (s32[16,128]{1,0:T(8,128)S(1)}, s32[16,128]{1,0:T(8,128)}, u32[]{:S(2)}) copy-start(s32[16,128]{1,0:T(8,128)} %box.1) | copy-start | bytes 24580

commit v3 on v2

v3 whole, which is shorter than its diff:
```python
import functools

import jax
import jax.numpy as jnp
from jax import lax
from jax.experimental import pallas as pl
from jax.experimental.pallas import tpu as pltpu
from jax.sharding import PartitionSpec as P

MESH = pl.DeviceIdType.MESH
F32 = jnp.float32
BF16 = jnp.bfloat16
LEV = 48
LANES = 128
PASSES = 4
NEAR = 2
CHUNK = 16


def two_terms(x):
    high = x.astype(BF16)
    return high, (x - high.astype(F32)).astype(BF16)


def mul(a, b):
    return jnp.dot(a, b, preferred_element_type=F32)


def mul_terms(a, b):
    a_high, a_low = two_terms(a)
    b_high, b_low = two_terms(b)
    return mul(a_high, b_high) + mul(a_high, b_low) + mul(a_low, b_high)


def lane_of(shape):
    return lax.broadcasted_iota(jnp.int32, shape, len(shape) - 1)


def kernel(
    nz,
    ng,
    count,
    vals_hbm,
    weight_hbm,
    box_hbm,
    owner_hbm,
    dx_hbm,
    dy_hbm,
    sp_hbm,
    land_hbm,
    corr_hbm,
    out_v,
    weight,
    box,
    owner,
    land,
    corr,
    vals,
    raw,
    ext,
    edge,
    pack_s,
    pack_r,
    slab_s,
    slab_r,
    sums_s,
    sums_r,
    by_level,
    part_s,
    part_r,
    tile_s,
    tile_r,
    box_s,
    box_r,
    field,
    face_below,
    local_sem,
    bulk_send,
    bulk_recv,
    pack_send,
    pack_recv,
    slab_send,
    slab_recv,
    all_send,
    all_recv,
    box_send,
    box_recv,
):
    group = 2 * ng
    per = LEV // ng
    rows1 = per * 8
    rows3 = tile_r.shape[1]
    sent3 = -(-per // 4) * 4
    owners = nz * ng
    depth = group * 8
    gx = lax.axis_index("gx")
    gy = lax.axis_index("gy")
    half = lax.div(gx, nz)
    z = lax.rem(gx, nz)
    me = half * ng + gy

    def member(step):
        index = lax.rem(me + step, group)
        h = lax.div(index, ng)
        g = lax.rem(index, ng)
        return index, h, g, (h * nz + z, g)

    def along_z(step):
        target = lax.rem(z + step, nz)
        return target, (half * nz + target, gy)

    east = (lax.rem(gx + 1, 2 * nz), gy)
    west = (lax.rem(gx + 2 * nz - 1, 2 * nz), gy)
    north = (gx, lax.rem(gy + 1, ng))
    south = (gx, lax.rem(gy + ng - 1, ng))

    def remote(src, dst, send, recv, device):
        return pltpu.make_async_remote_copy(
            src_ref=src,
            dst_ref=dst,
            send_sem=send,
            recv_sem=recv,
            device_id=device,
            device_id_type=MESH,
        )

    tile_r[...] = jnp.zeros(tile_r.shape, F32)
    tile_s[...] = jnp.zeros(tile_s.shape, F32)
    loads = [
        pltpu.make_async_copy(owner_hbm, owner, local_sem.at[0]),
        pltpu.make_async_copy(weight_hbm, weight, local_sem.at[1]),
        pltpu.make_async_copy(box_hbm, box, local_sem.at[2]),
        pltpu.make_async_copy(vals_hbm, vals, local_sem.at[3]),
        pltpu.make_async_copy(land_hbm, land, local_sem.at[4]),
        pltpu.make_async_copy(dx_hbm, raw.at[0], local_sem.at[5]),
        pltpu.make_async_copy(dy_hbm, raw.at[1], local_sem.at[6]),
        pltpu.make_async_copy(sp_hbm, raw.at[2], local_sem.at[7]),
        pltpu.make_async_copy(corr_hbm, corr, local_sem.at[8]),
    ]
    for load in loads[:4]:
        load.start()

    barrier = pltpu.get_barrier_semaphore()

    def greet_plane(step, _):
        pl.semaphore_signal(barrier, inc=1, device_id=member(step)[3], device_id_type=MESH)
        return _

    def greet_z(step, _):
        pl.semaphore_signal(barrier, inc=1, device_id=along_z(step)[1], device_id_type=MESH)
        return _

    lax.fori_loop(1, group, greet_plane, 0)
    lax.fori_loop(1, nz, greet_z, 0)
    for device in (east, west):
        pl.semaphore_signal(barrier, inc=1, device_id=device, device_id_type=MESH)
    for load in loads[4:]:
        load.start()

    for load in loads[:4]:
        load.wait()
    weighted = jnp.where(
        lax.broadcasted_iota(jnp.int32, (16, LANES), 0) < count[0], weight[...], 0.0
    )
    boxes = box[...]
    place = (boxes >> 6) * LANES + (boxes & 63)
    target = lax.broadcasted_iota(jnp.int32, (2 * LANES, LANES), 0)
    for j in range(8):
        terms = []
        hots = []
        for parity in range(2):
            b = 2 * j + parity
            value = vals[b].astype(F32) * weighted[b : b + 1, :]
            terms.append(two_terms(value))
            hit = target == place[b : b + 1, :] + 64 * parity
            hots.append(jnp.where(hit, 1.0, 0.0).astype(BF16))
        left = jnp.concatenate(
            [
                jnp.concatenate([terms[0][0], terms[1][0]], axis=1),
                jnp.concatenate([terms[0][1], terms[1][1]], axis=1),
            ],
            axis=0,
        )
        hot = jnp.concatenate(hots, axis=1)
        total = lax.dot_general(left, hot, (((1,), (1,)), ((), ())), preferred_element_type=F32)
        total = total[:LEV] + total[LEV:]
        by_level[0, pl.ds(j, LEV, stride=8), :] = total[:, :LANES]
        by_level[1, pl.ds(j, LEV, stride=8), :] = total[:, LANES:]

    lane1 = lane_of((1, LANES))
    base = lax.rem(me * 8, LANES)
    base_odd = lax.rem(me * 8 + 64, LANES)
    owner_row = jnp.zeros((1, LANES), F32)
    for j in range(8):
        owner_row = jnp.where(lane1 == base + j, owner[2 * j].astype(F32), owner_row)
        owner_row = jnp.where(lane1 == base_odd + j, owner[2 * j + 1].astype(F32), owner_row)
    for h in range(2):
        for g in range(ng):
            sums_s[h * ng + g, 0:rows1, :] = by_level[h, g * rows1 : (g + 1) * rows1, :]
            sums_s[h * ng + g, rows1 : rows1 + 1, :] = owner_row

    for load in loads[4:]:
        load.wait()
    mask = land[...].astype(F32)
    for x in range(8):
        for a in range(3):
            value = raw[a, pl.ds(x, LEV, stride=8), :]
            if a == 2:
                value = value * mask[x : x + 1, :]
            ext[4 + x, a] = value

    lane = lane_of((LEV, LANES))
    for part in range(2):
        to_south = jnp.zeros((LEV, LANES), F32)
        to_north = jnp.zeros((LEV, LANES), F32)
        for r in range(4):
            for a in range(3):
                q = 3 * r + a
                value = ext[4 + 4 * part + r, a]
                if q:
                    value = pltpu.roll(value, 8 * q, 1)
                low = (8 * q + LANES - 4) % LANES
                to_south = jnp.where((lane >= 8 * q) & (lane < 8 * q + 4), value, to_south)
                to_north = jnp.where((lane >= low) & (lane < low + 4), value, to_north)
        pack_s[0, part] = to_south
        pack_s[1, part] = to_north
    packs = [
        remote(pack_s.at[0], pack_r.at[0], pack_send.at[0], pack_recv.at[0], south),
        remote(pack_s.at[1], pack_r.at[1], pack_send.at[1], pack_recv.at[1], north),
    ]
    pl.semaphore_wait(barrier, group + nz)
    for copy in packs:
        copy.start()


    def send_sums(step, _):
        index, _, _, device = member(step)
        remote(
            sums_s.at[index], sums_r.at[me], all_send.at[0], all_recv.at[0], device
        ).start()
        return 0

    lax.fori_loop(1, group, send_sums, 0)
    sums_r[me] = sums_s[me]

    for copy in packs:
        copy.wait()
    for part in range(2):
        from_north = jnp.where(gy < ng - 1, pack_r[0, part], 0.0)
        from_south = jnp.where(gy > 0, pack_r[1, part], 0.0)
        slab_s[part] = jnp.where((lane & 7) < 4, from_north, from_south)
    slabs = [
        remote(slab_s.at[0], slab_r.at[1], slab_send.at[0], slab_recv.at[0], west),
        remote(slab_s.at[1], slab_r.at[0], slab_send.at[1], slab_recv.at[1], east),
    ]
    for copy in slabs:
        copy.start()
    def rows_to_neighbours(index, low, size):
        return [
            remote(
                ext.at[pl.ds(4 + low, size)],
                ext.at[pl.ds(12 + low, size)],
                bulk_send.at[index, 0],
                bulk_recv.at[index, 0],
                west,
            ),
            remote(
                ext.at[pl.ds(12 - low - size, size)],
                ext.at[pl.ds(4 - low - size, size)],
                bulk_send.at[index, 1],
                bulk_recv.at[index, 1],
                east,
            ),
        ]

    bulk = rows_to_neighbours(0, 0, NEAR)
    for copy in bulk:
        copy.start()

    level = lax.broadcasted_iota(jnp.int32, (LEV, ng * rows3), 0)
    column = lane_of((LEV, ng * rows3))
    from_group = column // rows3
    within = column - from_group * rows3
    chosen = (within < per) & (from_group * per + within == level)
    corr_v = corr[...]
    corr_rows = jnp.dot(
        corr_v,
        jnp.where(chosen, 1.0, 0.0),
        precision=lax.Precision.HIGHEST,
        preferred_element_type=F32,
    )

    for copy in slabs:
        copy.wait()
    outer = (lane < 4) | (lane >= LANES - 4)
    for part in range(4):
        slab = (slab_r[0], slab_s[0], slab_s[1], slab_r[1])[part]
        for r in range(4):
            for a in range(3):
                q = 3 * r + a
                value = pltpu.roll(slab, LANES - 8 * q, 1) if q else slab
                edge[4 * part + r, a] = jnp.where(outer, value, 0.0)

    def wait_bytes(ref, sem, size):
        view = ref.at[pl.ds(0, size)]
        pltpu.make_async_copy(view, view, sem).wait()

    wait_bytes(sums_r, all_recv.at[0], group - 1)
    wide = (depth + LANES - 1) // LANES
    owner_rows = []
    for parity in range(2):
        pieces = []
        for piece in range(wide):
            row = jnp.zeros((1, LANES), F32)
            for source in range(piece * 16, min(group, piece * 16 + 16)):
                start = (source * 8 + 64 * parity) % LANES
                row = jnp.where(
                    (lane1 >= start) & (lane1 < start + 8),
                    sums_r[source, rows1 : rows1 + 1, :],
                    row,
                )
            pieces.append(pltpu.roll(row, 64, 1) if parity else row)
        row = jnp.concatenate(pieces, axis=1) if wide > 1 else pieces[0]
        owner_rows.append(row[:, :depth])
    candidate = lax.broadcasted_iota(jnp.int32, (owners, depth), 0)
    even, odd = (row.astype(jnp.int32) for row in owner_rows)

    def hits(row, shift):
        return jnp.where(row == candidate + shift, 1.0, 0.0).astype(BF16)

    left = jnp.concatenate(
        [
            jnp.concatenate([hits(even, 0), hits(odd, 0)], axis=1),
            jnp.concatenate([hits(odd, owners), hits(even, owners)], axis=1),
        ],
        axis=0,
    )
    columns = []
    for t in range(per):
        value = sums_r[:, t * 8 : t * 8 + 8, :].reshape(depth, LANES)
        columns.append(jnp.concatenate([value, pltpu.roll(value, 64, 1)], axis=0))
    stack_high, stack_low = two_terms(jnp.concatenate(columns, axis=1))
    by_owner = mul(left, stack_high) + mul(left, stack_low)
    lower = lane_of((owners, LANES)) < 64
    for t in range(per):
        cut = by_owner[:, t * LANES : (t + 1) * LANES]
        part_s[:, t] = jnp.where(lower, cut[:owners], cut[owners:]).reshape(nz, ng, LANES)

    def send_parts(step, _):
        index, device = along_z(step)
        remote(
            part_s.at[index], part_r.at[z], all_send.at[1], all_recv.at[1], device
        ).start()
        return _

    lax.fori_loop(1, nz, send_parts, 0)
    part_r[z] = part_s[z]

    for copy in bulk:
        copy.wait()

    def faces(x, _):
        here, beyond = ext[x, 2], edge[x, 2]
        last = lane == LANES - 1
        turned, turned_beyond = pltpu.roll(here, LANES - 1, 1), pltpu.roll(beyond, LANES - 1, 1)
        ext[x, 0] = jnp.where(here * ext[x + 1, 2] > 0.0, ext[x, 0], 0.0)
        edge[x, 0] = jnp.where(beyond * edge[x + 1, 2] > 0.0, edge[x, 0], 0.0)
        upper = jnp.where(last, turned_beyond, turned)
        upper_beyond = jnp.where(last, turned, turned_beyond)
        north_face = jnp.where(here * upper > 0.0, ext[x, 1], 0.0)
        north_face_beyond = jnp.where(beyond * upper_beyond > 0.0, edge[x, 1], 0.0)
        turned, turned_beyond = pltpu.roll(north_face, 1, 1), pltpu.roll(north_face_beyond, 1, 1)
        ext[x, 1] = north_face
        edge[x, 1] = north_face_beyond
        face_below[x, 0] = jnp.where(lane == 0, turned_beyond, turned)
        face_below[x, 1] = jnp.where(lane == 0, turned, turned_beyond)
        return _

    lax.fori_loop(4 - NEAR, 11 + NEAR, faces, 0)

    wait_bytes(part_r, all_recv.at[1], nz - 1)
    row = lax.broadcasted_iota(jnp.int32, (ng, LANES), 0)
    box_column = lane_of((ng, LANES)) & 15
    low_boxes = lane_of((ng, LANES)) < 64
    for t in range(per):
        value = part_r[0, t]
        for source in range(1, nz):
            value = value + part_r[source, t]
        below = jnp.where(row == 0, 0.0, pltpu.roll(value, 1, 0))
        above = jnp.where(row == ng - 1, 0.0, pltpu.roll(value, ng - 1, 0))
        near = jnp.where(box_column == 15, below, above)
        other, other_near = pltpu.roll(value, 64, 1), pltpu.roll(near, 64, 1)
        tile_s[pl.ds(t, ng, stride=rows3), :] = jnp.where(low_boxes, value, other_near)
        tile_s[pl.ds(ng * rows3 + t, ng, stride=rows3), :] = jnp.where(low_boxes, other, near)

    def send_tiles(step, _):
        index, _, _, device = member(step)
        start = pl.multiple_of(index * rows3, 8)
        remote(
            tile_s.at[pl.ds(start, sent3)],
            tile_r.at[me, pl.ds(0, sent3)],
            all_send.at[2],
            all_recv.at[2],
            device,
        ).start()
        return 0

    lax.fori_loop(1, group, send_tiles, 0)
    far = rows_to_neighbours(1, NEAR, 4 - NEAR)
    for copy in far:
        copy.start()
    tile_r[me] = tile_s[pl.ds(pl.multiple_of(me * rows3, 8), rows3), :]

    wait_bytes(tile_r.at[:, pl.ds(0, sent3)], all_recv.at[2], group - 1)
    arrived = jnp.concatenate(
        [tile_r[h * ng : (h + 1) * ng].reshape(ng * rows3, LANES) for h in range(2)], axis=1
    )
    mixed = mul_terms(corr_rows, arrived)
    for h in range(2):
        box_s[h] = mixed[:, h * LANES : (h + 1) * LANES]
    borders = [
        remote(box_s.at[0], box_r.at[1], box_send.at[0], box_recv.at[0], west),
        remote(box_s.at[1], box_r.at[0], box_send.at[1], box_recv.at[1], east),
    ]
    for copy in borders:
        copy.start()
    for copy in far:
        copy.wait()
    lax.fori_loop(0, 4 - NEAR, faces, 0)
    lax.fori_loop(11 + NEAR, 15, faces, 0)
    for copy in borders:
        copy.wait()

    lane8 = lane_of((CHUNK, LANES))
    first, last = lane8 == 0, lane8 == LANES - 1

    def advance(step, _):
        rows = pl.ds(pl.multiple_of(step * CHUNK, 8), CHUNK)
        inner, outside = [], []
        for part in range(4):
            source = (box_r.at[0], box_s.at[0], box_s.at[1], box_r.at[1])[part]
            value = source[rows, :]
            for r in range(4):
                x = 4 * part + r
                at_inner = 16 * r + (lane8 >> 3)
                at_outside = jnp.where(lane8 < 64, 64 + 16 * r, 64 + 16 * r + 15)
                inner.append(ext[x, 2, rows, :] * jnp.take_along_axis(value, at_inner, axis=1))
                outside.append(
                    edge[x, 2, rows, :] * jnp.take_along_axis(value, at_outside, axis=1)
                )
        for turn in range(PASSES):
            low, high = 1 + turn, 15 - turn
            final = turn == PASSES - 1
            turned = {}
            for x in range(low, high):
                turned[x] = [
                    pltpu.roll(value[x], shift, 1)
                    for shift in (LANES - 1, 1)
                    for value in (inner, outside)
                ]
            flow = {}
            for x in range(low - 1, high):
                flow[x] = ext[x, 0, rows, :] * (inner[x + 1] - inner[x])
            new_inner, new_outside = list(inner), list(outside)
            for x in range(low, high):
                here = inner[x]
                above, above_beyond, below, below_beyond = turned[x]
                up = ext[x, 1, rows, :] * (jnp.where(last, above_beyond, above) - here)
                down = face_below[x, 0, rows, :] * (jnp.where(first, below_beyond, below) - here)
                new_inner[x] = here + (flow[x] - flow[x - 1]) + (up + down)
            if not final:
                for x in range(low - 1, high):
                    flow[x] = edge[x, 0, rows, :] * (outside[x + 1] - outside[x])
                for x in range(low, high):
                    here = outside[x]
                    above, above_beyond, below, below_beyond = turned[x]
                    up = edge[x, 1, rows, :] * (jnp.where(last, above, above_beyond) - here)
                    down = face_below[x, 1, rows, :] * (
                        jnp.where(first, below, below_beyond) - here
                    )
                    new_outside[x] = here + (flow[x] - flow[x - 1]) + (up + down)
            inner, outside = new_inner, new_outside
        for x in range(8):
            field[x, rows, :] = inner[4 + x]
        return _

    lax.fori_loop(0, LEV // CHUNK, advance, 0)

    whole = jnp.concatenate([field[x] for x in range(8)], axis=1)
    result = mul_terms(corr_v, whole)
    for x in range(8):
        out_v[pl.ds(x, LEV, stride=8), :] = ext[4 + x, 2] * result[:, x * LANES : (x + 1) * LANES]

    wait_bytes(sums_r, all_send.at[0], group - 1)
    wait_bytes(part_r, all_send.at[1], nz - 1)
    wait_bytes(tile_r.at[:, pl.ds(0, sent3)], all_send.at[2], group - 1)


def local(
    nz,
    ng,
    obs_values,
    obs_weight,
    obs_box,
    obs_owner,
    block_count,
    diff_x,
    diff_y,
    spread_std,
    land_sea,
    vert_corr,
):
    group = 2 * ng
    per = LEV // ng
    rows3 = -(-per // 8) * 8
    hbm = pl.BlockSpec(memory_space=pltpu.HBM)
    dma = pltpu.SemaphoreType.DMA
    flat = (LEV * 8, LANES)
    out = pl.pallas_call(
        functools.partial(kernel, nz, ng),
        out_shape=jax.ShapeDtypeStruct(flat, F32),
        in_specs=[pl.BlockSpec(memory_space=pltpu.SMEM)] + [hbm] * 9,
        out_specs=pl.BlockSpec(memory_space=pltpu.VMEM),
        scratch_shapes=[
            pltpu.VMEM((16, LANES), F32),
            pltpu.VMEM((16, LANES), jnp.int32),
            pltpu.SMEM((16,), jnp.int32),
            pltpu.VMEM((8, LANES), jnp.int32),
            pltpu.VMEM((LEV, LEV), F32),
            pltpu.VMEM((16, LEV, LANES), BF16),
            pltpu.VMEM((3,) + flat, F32),
            pltpu.VMEM((16, 3, LEV, LANES), F32),
            pltpu.VMEM((16, 3, LEV, LANES), F32),
            pltpu.VMEM((2, 2, LEV, LANES), F32),
            pltpu.VMEM((2, 2, LEV, LANES), F32),
            pltpu.VMEM((2, LEV, LANES), F32),
            pltpu.VMEM((2, LEV, LANES), F32),
            pltpu.VMEM((group, per * 8 + 1, LANES), F32),
            pltpu.VMEM((group, per * 8 + 1, LANES), F32),
            pltpu.VMEM((2,) + flat, F32),
            pltpu.VMEM((nz, per, ng, LANES), F32),
            pltpu.VMEM((nz, per, ng, LANES), F32),
            pltpu.VMEM((group * rows3, LANES), F32),
            pltpu.VMEM((group, rows3, LANES), F32),
            pltpu.VMEM((2, LEV, LANES), F32),
            pltpu.VMEM((2, LEV, LANES), F32),
            pltpu.VMEM((8, LEV, LANES), F32),
            pltpu.VMEM((16, 2, LEV, LANES), F32),
            dma((9,)),
            dma((2, 2)),
            dma((2, 2)),
            dma((2,)),
            dma((2,)),
            dma((2,)),
            dma((2,)),
            dma((3,)),
            dma((3,)),
            dma((2,)),
            dma((2,)),
        ],
        compiler_params=pltpu.CompilerParams(
            collective_id=0, has_side_effects=True, vmem_limit_bytes=40 * 1024 * 1024
        ),
        name="analysis",
    )(
        block_count,
        *(
            pltpu.with_memory_space_constraint(value, pltpu.HBM)
            for value in (
                obs_values,
                obs_weight,
                obs_box,
                obs_owner,
                diff_x.reshape(flat),
                diff_y.reshape(flat),
                spread_std.reshape(flat),
                land_sea,
                vert_corr,
            )
        ),
    )
    return out.reshape(LEV, 8, LANES)


def solution(mesh):
    in_specs = (
        P(("gx", "gy"), None, None),
        P(("gx", "gy"), None),
        P(("gx", "gy"), None),
        P(("gx", "gy")),
        P(("gx", "gy")),
        P(None, "gx", "gy"),
        P(None, "gx", "gy"),
        P(None, "gx", "gy"),
        P("gx", "gy"),
        P(),
    )
    return jax.shard_map(
        functools.partial(local, mesh.shape["gx"] // 2, mesh.shape["gy"]),
        mesh=mesh,
        in_specs=in_specs,
        out_specs=P(None, "gx", "gy"),
        check_vma=False,
    )
```

time: 52.5 us -> 38.6 us (0.74)
  Pallas kernels: 44.3 us -> 37 us
  local copies, waits for them, and re-layouts: 7.16 us -> 0.68 us
    pallas_call x1, Pallas kernels: 44.3 us -> 37 us  [local(): pl.pallas_call(functools.partial(kernel, nz, ng), out_shape=jax.ShapeDtyp...]
    unnamed x19 -> x1, local copies, waits for them, and re-layouts: 7.16 us -> 0.68 us
where the time goes in v3:
time: 38.6 us; the launch traced here: 38.3 us
  Pallas kernels  37 us (96%)
  local copies, waits for them, and re-layouts  0.68 us (2%)
  between operations  0.66 us (2%)
    pallas_call x1, Pallas kernels, local(): pl.pallas_call(functools.partial(kernel, nz, ng), out_shape=jax.ShapeDtyp...  37 us

profile of v3, /device:TPU:1, one launch (start us, length us, event | category | flops | bytes accessed | tf_op | source)
XLA Modules:
  0.0 38.3 jit_solution(9747377981248517626)
XLA Ops:
  0.7 37.0 %analysis.1 = f32[384,128]{1,0:T(8,128)S(1)} custom-call(s32[1]{0:T(128)S(6)} %copy.12.count, bf16[16,48,128]{2,1,0:T(8,128)(2,1)} %vals_hbm.1, f32[16,128]{1,0:T(8,128)} %weight_hbm.1, s32[16,128]{1,0:T(8,128)} %box_hbm.1, s32[16]{0:T(128)} %owner_hbm.1, f32[384,128]{1,0:T(8,128)} %bitcast.5, f32[384,128]{1,0:T(8,128)} %bitcast.6, f32[384,128]{1,0:T(8,128)} %bitcast.7, ...), custom_call_target="tpu_custom_call" | custom-call | tf_op jit(solution)/shard_map/analysis/pallas_call | solution.py:519
  37.7 0.7 %copy.13 = f32[48,8,128]{2,1,0:T(8,128)} copy(f32[48,8,128]{2,1,0:T(8,128)S(1)} %bitcast.4) | data formatting | bytes 393216

commit v4 on v3

--- a/solution.py
+++ b/solution.py
@@ -89,6 +89,9 @@
     group = 2 * ng
     per = LEV // ng
     rows1 = per * 8
+    late = per // 3
+    early = per - late
+    late8 = late * 8
     rows3 = tile_r.shape[1]
     sent3 = -(-per // 4) * 4
     owners = nz * ng
@@ -99,11 +102,33 @@
     z = lax.rem(gx, nz)
     me = half * ng + gy
 
-    def member(step):
-        index = lax.rem(me + step, group)
-        h = lax.div(index, ng)
-        g = lax.rem(index, ng)
-        return index, h, g, (h * nz + z, g)
+    nx = ng // 4
+    y = 2 * lax.div(gy, ng // 2) + half
+    x_core = lax.rem(gy, ng // 2)
+    chip_x, core = lax.div(x_core, 2), lax.rem(x_core, 2)
+
+    def hops(step, size):
+        return min(step, size - step)
+
+    offsets = sorted(
+        (
+            (oy, ox, oc)
+            for oy in range(4)
+            for ox in range(nx)
+            for oc in range(2)
+            if oy or ox or oc
+        ),
+        key=lambda o: (-hops(o[0], 4) - hops(o[1], nx), o[2], (o[0] + o[1]) % 4, o),
+    )
+    z_steps = sorted(range(1, nz), key=lambda step: (-hops(step, nz), step))
+
+    def member(offset):
+        to_y = lax.rem(y + offset[0], 4)
+        to_x = lax.rem(chip_x + offset[1], nx)
+        to_core = lax.rem(core + offset[2], 2)
+        h = lax.rem(to_y, 2)
+        g = lax.div(to_y, 2) * (ng // 2) + 2 * to_x + to_core
+        return h * ng + g, (h * nz + z, g)
 
     def along_z(step):
         target = lax.rem(z + step, nz)
@@ -142,17 +167,12 @@
 
     barrier = pltpu.get_barrier_semaphore()
 
-    def greet_plane(step, _):
-        pl.semaphore_signal(barrier, inc=1, device_id=member(step)[3], device_id_type=MESH)
-        return _
-
-    def greet_z(step, _):
-        pl.semaphore_signal(barrier, inc=1, device_id=along_z(step)[1], device_id_type=MESH)
-        return _
-
-    lax.fori_loop(1, group, greet_plane, 0)
-    lax.fori_loop(1, nz, greet_z, 0)
-    for device in (east, west):
+    for device in (
+        *(member(offset)[1] for offset in offsets),
+        *(along_z(step)[1] for step in z_steps),
+        east,
+        west,
+    ):
         pl.semaphore_signal(barrier, inc=1, device_id=device, device_id_type=MESH)
     for load in loads[4:]:
         load.start()
@@ -196,7 +216,9 @@
         owner_row = jnp.where(lane1 == base_odd + j, owner[2 * j + 1].astype(F32), owner_row)
     for h in range(2):
         for g in range(ng):
-            sums_s[h * ng + g, 0:rows1, :] = by_level[h, g * rows1 : (g + 1) * rows1, :]
+            low = g * rows1
+            sums_s[h * ng + g, late8:rows1, :] = by_level[h, low : low + rows1 - late8, :]
+            sums_s[h * ng + g, 0:late8, :] = by_level[h, low + rows1 - late8 : low + rows1, :]
             sums_s[h * ng + g, rows1 : rows1 + 1, :] = owner_row
 
     for load in loads[4:]:
@@ -233,14 +255,18 @@
         copy.start()
 
 
-    def send_sums(step, _):
-        index, _, _, device = member(step)
-        remote(
-            sums_s.at[index], sums_r.at[me], all_send.at[0], all_recv.at[0], device
-        ).start()
-        return 0
-
-    lax.fori_loop(1, group, send_sums, 0)
+    early_rows = pl.ds(late8, rows1 + 1 - late8)
+    late_rows = pl.ds(0, late8)
+    for k, rows in enumerate((early_rows, late_rows)):
+        for offset in offsets:
+            index, device = member(offset)
+            remote(
+                sums_s.at[index, rows],
+                sums_r.at[me, rows],
+                all_send.at[k],
+                all_recv.at[k],
+                device,
+            ).start()
     sums_r[me] = sums_s[me]
 
     for copy in packs:
@@ -305,7 +331,7 @@
         view = ref.at[pl.ds(0, size)]
         pltpu.make_async_copy(view, view, sem).wait()
 
-    wait_bytes(sums_r, all_recv.at[0], group - 1)
+    wait_bytes(sums_r.at[:, early_rows], all_recv.at[0], group - 1)
     wide = (depth + LANES - 1) // LANES
     owner_rows = []
     for parity in range(2):
@@ -335,25 +361,35 @@
         ],
         axis=0,
     )
-    columns = []
-    for t in range(per):
-        value = sums_r[:, t * 8 : t * 8 + 8, :].reshape(depth, LANES)
-        columns.append(jnp.concatenate([value, pltpu.roll(value, 64, 1)], axis=0))
-    stack_high, stack_low = two_terms(jnp.concatenate(columns, axis=1))
-    by_owner = mul(left, stack_high) + mul(left, stack_low)
     lower = lane_of((owners, LANES)) < 64
-    for t in range(per):
-        cut = by_owner[:, t * LANES : (t + 1) * LANES]
-        part_s[:, t] = jnp.where(lower, cut[:owners], cut[owners:]).reshape(nz, ng, LANES)
-
-    def send_parts(step, _):
-        index, device = along_z(step)
-        remote(
-            part_s.at[index], part_r.at[z], all_send.at[1], all_recv.at[1], device
-        ).start()
-        return _
-
-    lax.fori_loop(1, nz, send_parts, 0)
+
+    def add_by_owner(k, first_level, levels, first_row):
+        columns = []
+        for t in range(levels):
+            low = first_row + 8 * t
+            value = sums_r[:, low : low + 8, :].reshape(depth, LANES)
+            columns.append(jnp.concatenate([value, pltpu.roll(value, 64, 1)], axis=0))
+        stack_high, stack_low = two_terms(jnp.concatenate(columns, axis=1))
+        by_owner = mul(left, stack_high) + mul(left, stack_low)
+        for t in range(levels):
+            cut = by_owner[:, t * LANES : (t + 1) * LANES]
+            part_s[:, first_level + t] = jnp.where(
+                lower, cut[:owners], cut[owners:]
+            ).reshape(nz, ng, LANES)
+        for step in z_steps:
+            index, device = along_z(step)
+            chosen_levels = pl.ds(first_level, levels)
+            remote(
+                part_s.at[index, chosen_levels],
+                part_r.at[z, chosen_levels],
+                all_send.at[2 + k],
+                all_recv.at[2 + k],
+                device,
+            ).start()
+
+    add_by_owner(0, 0, early, late8)
+    wait_bytes(sums_r.at[:, late_rows], all_recv.at[1], group - 1)
+    add_by_owner(1, early, late, 0)
     part_r[z] = part_s[z]
 
     for copy in bulk:
@@ -378,7 +414,12 @@
 
     lax.fori_loop(4 - NEAR, 11 + NEAR, faces, 0)
 
-    wait_bytes(part_r, all_recv.at[1], nz - 1)
+    parts = [
+        (part_r.at[:, pl.ds(0, early)], 2),
+        (part_r.at[:, pl.ds(early, late)], 3),
+    ]
+    for ref, k in parts:
+        wait_bytes(ref, all_recv.at[k], nz - 1)
     row = lax.broadcasted_iota(jnp.int32, (ng, LANES), 0)
     box_column = lane_of((ng, LANES)) & 15
     low_boxes = lane_of((ng, LANES)) < 64
@@ -393,25 +434,23 @@
         tile_s[pl.ds(t, ng, stride=rows3), :] = jnp.where(low_boxes, value, other_near)
         tile_s[pl.ds(ng * rows3 + t, ng, stride=rows3), :] = jnp.where(low_boxes, other, near)
 
-    def send_tiles(step, _):
-        index, _, _, device = member(step)
+    first_rows = pl.ds(0, sent3)
+    for offset in offsets:
+        index, device = member(offset)
         start = pl.multiple_of(index * rows3, 8)
         remote(
             tile_s.at[pl.ds(start, sent3)],
-            tile_r.at[me, pl.ds(0, sent3)],
-            all_send.at[2],
-            all_recv.at[2],
+            tile_r.at[me, first_rows],
+            all_send.at[4],
+            all_recv.at[4],
             device,
         ).start()
-        return 0
-
-    lax.fori_loop(1, group, send_tiles, 0)
     far = rows_to_neighbours(1, NEAR, 4 - NEAR)
     for copy in far:
         copy.start()
     tile_r[me] = tile_s[pl.ds(pl.multiple_of(me * rows3, 8), rows3), :]
 
-    wait_bytes(tile_r.at[:, pl.ds(0, sent3)], all_recv.at[2], group - 1)
+    wait_bytes(tile_r.at[:, first_rows], all_recv.at[4], group - 1)
     arrived = jnp.concatenate(
         [tile_r[h * ng : (h + 1) * ng].reshape(ng * rows3, LANES) for h in range(2)], axis=1
     )
@@ -491,9 +530,11 @@
     for x in range(8):
         out_v[pl.ds(x, LEV, stride=8), :] = ext[4 + x, 2] * result[:, x * LANES : (x + 1) * LANES]
 
-    wait_bytes(sums_r, all_send.at[0], group - 1)
-    wait_bytes(part_r, all_send.at[1], nz - 1)
-    wait_bytes(tile_r.at[:, pl.ds(0, sent3)], all_send.at[2], group - 1)
+    wait_bytes(sums_r.at[:, early_rows], all_send.at[0], group - 1)
+    wait_bytes(sums_r.at[:, late_rows], all_send.at[1], group - 1)
+    for ref, k in parts:
+        wait_bytes(ref, all_send.at[k], nz - 1)
+    wait_bytes(tile_r.at[:, first_rows], all_send.at[4], group - 1)
 
 
 def local(
@@ -553,8 +594,8 @@
             dma((2,)),
             dma((2,)),
             dma((2,)),
-            dma((3,)),
-            dma((3,)),
+            dma((5,)),
+            dma((5,)),
             dma((2,)),
             dma((2,)),
         ],

time: 38.6 us -> 37.1 us (0.961)
  Pallas kernels: 37 us -> 35.6 us
    pallas_call x1, Pallas kernels: 37 us -> 35.6 us  [local(): pl.pallas_call(functools.partial(kernel, nz, ng), out_shape=jax.ShapeDtyp...]
where the time goes in v4:
time: 37.1 us; the launch traced here: 37 us
  Pallas kernels  35.6 us (96%)
  local copies, waits for them, and re-layouts  0.68 us (2%)
  between operations  0.66 us (2%)
    pallas_call x1, Pallas kernels, local(): pl.pallas_call(functools.partial(kernel, nz, ng), out_shape=jax.ShapeDtyp...  35.6 us

profile of v4, /device:TPU:1, one launch (start us, length us, event | category | flops | bytes accessed | tf_op | source)
XLA Modules:
  0.0 37.0 jit_solution(14645363363942441139)
XLA Ops:
  0.7 35.6 %analysis.1 = f32[384,128]{1,0:T(8,128)S(1)} custom-call(s32[1]{0:T(128)S(6)} %copy.12.count, bf16[16,48,128]{2,1,0:T(8,128)(2,1)} %vals_hbm.1, f32[16,128]{1,0:T(8,128)} %weight_hbm.1, s32[16,128]{1,0:T(8,128)} %box_hbm.1, s32[16]{0:T(128)} %owner_hbm.1, f32[384,128]{1,0:T(8,128)} %bitcast.5, f32[384,128]{1,0:T(8,128)} %bitcast.6, f32[384,128]{1,0:T(8,128)} %bitcast.7, ...), custom_call_target="tpu_custom_call" | custom-call | tf_op jit(solution)/shard_map/analysis/pallas_call | solution.py:560
  36.3 0.7 %copy.13 = f32[48,8,128]{2,1,0:T(8,128)} copy(f32[48,8,128]{2,1,0:T(8,128)S(1)} %bitcast.4) | data formatting | bytes 393216

commit v5 on v4

--- a/solution.py
+++ b/solution.py
@@ -15,6 +15,7 @@
 PASSES = 4
 NEAR = 2
 CHUNK = 16
+CHUNK_END = 24
 
 
 def two_terms(x):
@@ -74,6 +75,7 @@
     box_r,
     field,
     face_below,
+    ready,
     local_sem,
     bulk_send,
     bulk_recv,
@@ -463,67 +465,93 @@
     ]
     for copy in borders:
         copy.start()
+
+    def levels_of(step, size):
+        rows = pl.ds(pl.multiple_of(step * size, 8), size)
+        lanes = lane_of((size, LANES))
+        first, last = lanes == 0, lanes == LANES - 1
+
+        def forced(part, source):
+            value = source[rows, :]
+            made = {}
+            for r in range(4):
+                x = 4 * part + r
+                at_inner = 16 * r + (lanes >> 3)
+                at_outside = jnp.where(lanes < 64, 64 + 16 * r, 64 + 16 * r + 15)
+                made[x] = (
+                    ext[x, 2, rows, :] * jnp.take_along_axis(value, at_inner, axis=1),
+                    edge[x, 2, rows, :] * jnp.take_along_axis(value, at_outside, axis=1),
+                )
+            return made
+
+        def passed(turn, chosen, state):
+            needed = sorted({x - 1 for x in chosen} | set(chosen))
+            turned = {
+                x: [pltpu.roll(state[x][k], shift, 1) for shift in (LANES - 1, 1) for k in range(2)]
+                for x in chosen
+            }
+            result = {x: [None, None] for x in chosen}
+            for k, faces_of in enumerate((ext, edge)):
+                if k and turn == PASSES - 1:
+                    break
+                flow = {
+                    x: faces_of[x, 0, rows, :] * (state[x + 1][k] - state[x][k]) for x in needed
+                }
+                for x in chosen:
+                    here = state[x][k]
+                    above, below = turned[x][:2], turned[x][2:]
+                    up = faces_of[x, 1, rows, :] * (
+                        jnp.where(last, above[1 - k], above[k]) - here
+                    )
+                    down = face_below[x, k, rows, :] * (
+                        jnp.where(first, below[1 - k], below[k]) - here
+                    )
+                    result[x][k] = here + (flow[x] - flow[x - 1]) + (up + down)
+            return result
+
+        return rows, forced, passed
+
+    def begin(step, _):
+        rows, forced, passed = levels_of(step, CHUNK)
+        state = {**forced(1, box_s.at[0]), **forced(2, box_s.at[1])}
+        for turn in range(PASSES):
+            for x in state:
+                for k in range(2):
+                    ready[turn, x - 4, k, rows, :] = state[x][k]
+            if turn < PASSES - 1:
+                state = passed(turn, range(5 + turn, 11 - turn), state)
+        return _
+
+    def finish(step, _):
+        rows, forced, passed = levels_of(step, CHUNK_END)
+
+        def known(turn):
+            return {
+                x: [ready[turn, x - 4, k, rows, :] for k in range(2)]
+                for x in range(4 + turn, 12 - turn)
+            }
+
+        state = {**forced(0, box_r.at[0]), **known(0), **forced(3, box_r.at[1])}
+        for turn in range(PASSES):
+            chosen = [
+                x
+                for x in range(1 + turn, 15 - turn)
+                if turn == PASSES - 1 or not 5 + turn <= x < 11 - turn
+            ]
+            new = passed(turn, chosen, state)
+            state = new if turn == PASSES - 1 else {**new, **known(turn + 1)}
+        for x in range(8):
+            field[x, rows, :] = state[4 + x][0]
+        return _
+
+    lax.fori_loop(0, LEV // CHUNK, begin, 0)
     for copy in far:
         copy.wait()
     lax.fori_loop(0, 4 - NEAR, faces, 0)
     lax.fori_loop(11 + NEAR, 15, faces, 0)
     for copy in borders:
         copy.wait()
-
-    lane8 = lane_of((CHUNK, LANES))
-    first, last = lane8 == 0, lane8 == LANES - 1
-
-    def advance(step, _):
-        rows = pl.ds(pl.multiple_of(step * CHUNK, 8), CHUNK)
-        inner, outside = [], []
-        for part in range(4):
-            source = (box_r.at[0], box_s.at[0], box_s.at[1], box_r.at[1])[part]
-            value = source[rows, :]
-            for r in range(4):
-                x = 4 * part + r
-                at_inner = 16 * r + (lane8 >> 3)
-                at_outside = jnp.where(lane8 < 64, 64 + 16 * r, 64 + 16 * r + 15)
-                inner.append(ext[x, 2, rows, :] * jnp.take_along_axis(value, at_inner, axis=1))
-                outside.append(
-                    edge[x, 2, rows, :] * jnp.take_along_axis(value, at_outside, axis=1)
-                )
-        for turn in range(PASSES):
-            low, high = 1 + turn, 15 - turn
-            final = turn == PASSES - 1
-            turned = {}
-            for x in range(low, high):
-                turned[x] = [
-                    pltpu.roll(value[x], shift, 1)
-                    for shift in (LANES - 1, 1)
-                    for value in (inner, outside)
-                ]
-            flow = {}
-            for x in range(low - 1, high):
-                flow[x] = ext[x, 0, rows, :] * (inner[x + 1] - inner[x])
-            new_inner, new_outside = list(inner), list(outside)
-            for x in range(low, high):
-                here = inner[x]
-                above, above_beyond, below, below_beyond = turned[x]
-                up = ext[x, 1, rows, :] * (jnp.where(last, above_beyond, above) - here)
-                down = face_below[x, 0, rows, :] * (jnp.where(first, below_beyond, below) - here)
-                new_inner[x] = here + (flow[x] - flow[x - 1]) + (up + down)
-            if not final:
-                for x in range(low - 1, high):
-                    flow[x] = edge[x, 0, rows, :] * (outside[x + 1] - outside[x])
-                for x in range(low, high):
-                    here = outside[x]
-                    above, above_beyond, below, below_beyond = turned[x]
-                    up = edge[x, 1, rows, :] * (jnp.where(last, above, above_beyond) - here)
-                    down = face_below[x, 1, rows, :] * (
-                        jnp.where(first, below, below_beyond) - here
-                    )
-                    new_outside[x] = here + (flow[x] - flow[x - 1]) + (up + down)
-            inner, outside = new_inner, new_outside
-        for x in range(8):
-            field[x, rows, :] = inner[4 + x]
-        return _
-
-    lax.fori_loop(0, LEV // CHUNK, advance, 0)
+    lax.fori_loop(0, LEV // CHUNK_END, finish, 0)
 
     whole = jnp.concatenate([field[x] for x in range(8)], axis=1)
     result = mul_terms(corr_v, whole)
@@ -587,6 +615,7 @@
             pltpu.VMEM((2, LEV, LANES), F32),
             pltpu.VMEM((8, LEV, LANES), F32),
             pltpu.VMEM((16, 2, LEV, LANES), F32),
+            pltpu.VMEM((PASSES, 8, 2, LEV, LANES), F32),
             dma((9,)),
             dma((2, 2)),
             dma((2, 2)),

time: 37.1 us -> 36.6 us (0.987)
  Pallas kernels: 35.6 us -> 35.1 us
    pallas_call x1, Pallas kernels: 35.6 us -> 35.1 us  [local(): pl.pallas_call(functools.partial(kernel, nz, ng), out_shape=jax.ShapeDtyp...]
where the time goes in v5:
time: 36.6 us; the launch traced here: 36.5 us
  Pallas kernels  35.1 us (96%)
  local copies, waits for them, and re-layouts  0.68 us (2%)
  between operations  0.66 us (2%)
    pallas_call x1, Pallas kernels, local(): pl.pallas_call(functools.partial(kernel, nz, ng), out_shape=jax.ShapeDtyp...  35.1 us

profile of v5, /device:TPU:1, one launch (start us, length us, event | category | flops | bytes accessed | tf_op | source)
XLA Modules:
  0.0 36.5 jit_solution(24300136270691328)
XLA Ops:
  0.7 35.1 %analysis.1 = f32[384,128]{1,0:T(8,128)S(1)} custom-call(s32[1]{0:T(128)S(6)} %copy.12.count, bf16[16,48,128]{2,1,0:T(8,128)(2,1)} %vals_hbm.1, f32[16,128]{1,0:T(8,128)} %weight_hbm.1, s32[16,128]{1,0:T(8,128)} %box_hbm.1, s32[16]{0:T(128)} %owner_hbm.1, f32[384,128]{1,0:T(8,128)} %bitcast.5, f32[384,128]{1,0:T(8,128)} %bitcast.6, f32[384,128]{1,0:T(8,128)} %bitcast.7, ...), custom_call_target="tpu_custom_call" | custom-call | tf_op jit(solution)/shard_map/analysis/pallas_call | solution.py:588
  35.8 0.7 %copy.13 = f32[48,8,128]{2,1,0:T(8,128)} copy(f32[48,8,128]{2,1,0:T(8,128)S(1)} %bitcast.4) | data formatting | bytes 393216

commit v6 on v5

--- a/solution.py
+++ b/solution.py
@@ -15,7 +15,7 @@
 PASSES = 4
 NEAR = 2
 CHUNK = 16
-CHUNK_END = 24
+CHUNK_END = 48
 
 
 def two_terms(x):
@@ -420,12 +420,13 @@
         (part_r.at[:, pl.ds(0, early)], 2),
         (part_r.at[:, pl.ds(early, late)], 3),
     ]
-    for ref, k in parts:
-        wait_bytes(ref, all_recv.at[k], nz - 1)
+    wait_bytes(parts[0][0], all_recv.at[2], nz - 1)
     row = lax.broadcasted_iota(jnp.int32, (ng, LANES), 0)
     box_column = lane_of((ng, LANES)) & 15
     low_boxes = lane_of((ng, LANES)) < 64
     for t in range(per):
+        if t == early:
+            wait_bytes(parts[1][0], all_recv.at[3], nz - 1)
         value = part_r[0, t]
         for source in range(1, nz):
             value = value + part_r[source, t]

time: 36.6 us -> 36.4 us (level)
  no operation moved by 1% of the time
where the time goes in v6:
time: 36.4 us; the launch traced here: 36.3 us
  Pallas kernels  35 us (96%)
  local copies, waits for them, and re-layouts  0.68 us (2%)
  between operations  0.66 us (2%)
    pallas_call x1, Pallas kernels, local(): pl.pallas_call(functools.partial(kernel, nz, ng), out_shape=jax.ShapeDtyp...  35 us

profile of v6, /device:TPU:1, one launch (start us, length us, event | category | flops | bytes accessed | tf_op | source)
XLA Modules:
  0.0 36.3 jit_solution(10706257049207826206)
XLA Ops:
  0.7 35.0 %analysis.1 = f32[384,128]{1,0:T(8,128)S(1)} custom-call(s32[1]{0:T(128)S(6)} %copy.12.count, bf16[16,48,128]{2,1,0:T(8,128)(2,1)} %vals_hbm.1, f32[16,128]{1,0:T(8,128)} %weight_hbm.1, s32[16,128]{1,0:T(8,128)} %box_hbm.1, s32[16]{0:T(128)} %owner_hbm.1, f32[384,128]{1,0:T(8,128)} %bitcast.5, f32[384,128]{1,0:T(8,128)} %bitcast.6, f32[384,128]{1,0:T(8,128)} %bitcast.7, ...), custom_call_target="tpu_custom_call" | custom-call | tf_op jit(solution)/shard_map/analysis/pallas_call | solution.py:589
  35.6 0.7 %copy.13 = f32[48,8,128]{2,1,0:T(8,128)} copy(f32[48,8,128]{2,1,0:T(8,128)S(1)} %bitcast.4) | data formatting | bytes 393216

commit v7 on v6

--- a/solution.py
+++ b/solution.py
@@ -79,6 +79,8 @@
     local_sem,
     bulk_send,
     bulk_recv,
+    edge_send,
+    edge_recv,
     pack_send,
     pack_recv,
     slab_send,
@@ -448,7 +450,15 @@
             all_recv.at[4],
             device,
         ).start()
-    far = rows_to_neighbours(1, NEAR, 4 - NEAR)
+    far = rows_to_neighbours(1, NEAR, 3 - NEAR)
+    for k, (source, target, device) in enumerate(
+        (
+            (ext.at[7, 2], ext.at[15, 2], west),
+            (ext.at[8, 0], ext.at[0, 0], east),
+            (ext.at[8, 2], ext.at[0, 2], east),
+        )
+    ):
+        far.append(remote(source, target, edge_send.at[k], edge_recv.at[k], device))
     for copy in far:
         copy.start()
     tile_r[me] = tile_s[pl.ds(pl.multiple_of(me * rows3, 8), rows3), :]
@@ -620,6 +630,8 @@
             dma((9,)),
             dma((2, 2)),
             dma((2, 2)),
+            dma((3,)),
+            dma((3,)),
             dma((2,)),
             dma((2,)),
             dma((2,)),

time: 36.4 us -> 36.3 us (level)
  no operation moved by 1% of the time
where the time goes in v7:
time: 36.3 us; the launch traced here: 36.2 us
  Pallas kernels  34.9 us (96%)
  local copies, waits for them, and re-layouts  0.68 us (2%)
  between operations  0.66 us (2%)
    pallas_call x1, Pallas kernels, local(): pl.pallas_call(functools.partial(kernel, nz, ng), out_shape=jax.ShapeDtyp...  34.9 us

profile of v7, /device:TPU:1, one launch (start us, length us, event | category | flops | bytes accessed | tf_op | source)
XLA Modules:
  0.0 36.2 jit_solution(9122469737954726549)
XLA Ops:
  0.7 34.9 %analysis.1 = f32[384,128]{1,0:T(8,128)S(1)} custom-call(s32[1]{0:T(128)S(6)} %copy.12.count, bf16[16,48,128]{2,1,0:T(8,128)(2,1)} %vals_hbm.1, f32[16,128]{1,0:T(8,128)} %weight_hbm.1, s32[16,128]{1,0:T(8,128)} %box_hbm.1, s32[16]{0:T(128)} %owner_hbm.1, f32[384,128]{1,0:T(8,128)} %bitcast.5, f32[384,128]{1,0:T(8,128)} %bitcast.6, f32[384,128]{1,0:T(8,128)} %bitcast.7, ...), custom_call_target="tpu_custom_call" | custom-call | tf_op jit(solution)/shard_map/analysis/pallas_call | solution.py:599
  35.5 0.7 %copy.13 = f32[48,8,128]{2,1,0:T(8,128)} copy(f32[48,8,128]{2,1,0:T(8,128)S(1)} %bitcast.4) | data formatting | bytes 393216
